TPU v7x, 32 devices: a whole 2x2x4 slice. The times are simulated.
32 devices in a mesh: slab: 8 (over z, y), grp: 4 (over x, core).
Axes of the slice: x: 2, y: 2, z: 4, core: 2. Of those that a mesh axis runs over, the one named last changes fastest.
Arguments:
- u_now: float32 [3, 128, 32, 128], P(None, 'slab', 'grp'), may hold values from -6 to 6
- u_prev: float32 [3, 128, 32, 128], P(None, 'slab', 'grp'), may hold values from -6 to 6
- force: float32 [3, 128, 32, 128], P(None, 'slab', 'grp'), may hold values from -6 to 6
- stiffness: float32 [128, 32, 128], P('slab', 'grp'), may hold values from 0.5 to 2
- broken: int32 [32, 8, 32], P('slab', 'grp'), may hold values 0 or 1
- flags: int32 [32, 8, 32], P('slab', 'grp'), may hold values 0 or 1
Outputs:
- displacement: float32 [3, 128, 32, 128], P(None, 'slab', 'grp')
- coeffs: float32 [6, 32, 128, 128], P(None, 'grp', 'slab')
All inputs are finite; a program needn't handle non-finite values. No bound on the sum of `broken` or of `flags` on one device may be relied on, other than what follows from the above.
Results may differ from a plain program's by a relative error of at most 0.0001.
Values sent between devices are 32-bit elements; how exact they have to be, the bound alone decides.
A program may use at most 64 MiB of HBM per device.

v0:
```python
import jax
import jax.numpy as jnp
import numpy as np
from jax import lax
from jax.experimental import pallas as pl
from jax.experimental.pallas import tpu as pltpu
from jax.sharding import PartitionSpec as P

STEPS = 2
ITERS = 2
LEVELS = 3


SPRING_NORMAL = 1.0
SPRING_SHEAR = 0.4
MASS_TERM = 1.0
CRACK_CUT = 0.9


def with_halo(block, sides, width):
    for axis, dim in sides:
        count = lax.axis_size(axis)
        forward = [(i, i + 1) for i in range(count - 1)]
        backward = [(target, source) for source, target in forward]
        low = lax.ppermute(
            lax.slice_in_dim(block, block.shape[dim] - width, None, axis=dim), axis, forward
        )
        high = lax.ppermute(lax.slice_in_dim(block, 0, width, axis=dim), axis, backward)
        block = jnp.concatenate([low, block, high], axis=dim)
    return block


def cosine_table():
    freq = np.arange(4)[:, None]
    place = np.arange(4)[None, :]
    factor = np.where(freq == 0, 0.5, np.sqrt(0.5))
    return factor * np.cos(np.pi * (2 * place + 1) * freq / 8.0)


def block_table(count):
    return jnp.asarray(np.kron(np.eye(count // 4), cosine_table()), jnp.float32)


def spread(mask):
    values = mask.astype(jnp.float32)
    size_a, size_b, size_c = values.shape
    wide = jnp.broadcast_to(values[:, None, :, None, :, None], (size_a, 4, size_b, 4, size_c, 4))
    return wide.reshape(size_a * 4, size_b * 4, size_c * 4)


def sides(padded, axis_index):
    leading = padded.ndim - 3

    def cut(offset):
        index_list = [slice(None)] * leading + [slice(1, -1)] * 3
        length = padded.shape[leading + axis_index]
        index_list[leading + axis_index] = slice(1 + offset, length - 1 + offset)
        return padded[tuple(index_list)]

    return (cut(1), cut(-1))


def springs(field, weight, field_pad, weight_pad):
    result = MASS_TERM * field
    for axis_index in range(3):
        upper_v, lower_v = sides(field_pad, axis_index)
        upper_w, lower_w = sides(weight_pad, axis_index)
        k_upper = 0.5 * (weight + upper_w)
        k_lower = 0.5 * (weight + lower_w)
        change = k_upper * (field - upper_v) + k_lower * (field - lower_v)
        coupling = jnp.array(
            [SPRING_NORMAL if comp == axis_index else SPRING_SHEAR for comp in range(3)],
            jnp.float32,
        ).reshape(3, 1, 1, 1)
        result = result + coupling * change
    return result


def faces(field):
    padded = with_halo(field, (("slab", 1), ("grp", 2)), 1)
    return jnp.pad(padded, ((0, 0), (0, 0), (0, 0), (1, 1)))


def stresses(carry, field_pad):
    rows_out = []
    for axis_index in range(3):
        upper_v, lower_v = sides(field_pad, axis_index)
        rows_out.append(SPRING_NORMAL * carry * 0.5 * (upper_v[axis_index] - lower_v[axis_index]))
    return jnp.stack(rows_out)


def paired_sum(residual, image):
    return lax.psum((jnp.sum(residual * residual), jnp.sum(residual * image)), ("slab", "grp"))


def lift(signal):
    even = signal[..., 0::2]
    odd = signal[..., 1::2]
    detail = odd - 0.5 * (even + jnp.roll(even, -1, axis=-1))
    approx = even + 0.25 * (jnp.roll(detail, 1, axis=-1) + detail)
    return (approx, detail)


def wavelet(signal):
    pieces = []
    approx = signal
    for level_index in range(LEVELS):
        approx, detail = lift(approx)
        pieces.insert(0, detail)
    return jnp.concatenate([approx] + pieces, axis=-1)


def body(u_now, u_prev, force, stiffness, broken, flags):
    weight = stiffness * (1.0 - CRACK_CUT * spread(broken))
    carry = spread(flags) * weight
    weight_pad = with_halo(weight, (("slab", 0), ("grp", 1)), 1)
    weight_pad = jnp.pad(weight_pad, ((0, 0), (0, 0), (1, 1)))

    def operate(field):
        return springs(field, weight, faces(field), weight_pad)

    for step_index in range(STEPS):
        rhs = MASS_TERM * (2.0 * u_now - u_prev) + force
        guess = u_now
        residual = rhs - operate(guess)
        image = operate(residual)
        norm_now, product = paired_sum(residual, image)
        alpha = norm_now / product
        direction, along = (residual, image)
        for turn_index in range(ITERS):
            guess = guess + alpha * direction
            residual = residual - alpha * along
            if turn_index + 1 < ITERS:
                image = operate(residual)
                norm_next, product = paired_sum(residual, image)
                ratio = norm_next / norm_now
                alpha = norm_next / (product - ratio * norm_next / alpha)
                direction = residual + ratio * direction
                along = image + ratio * along
                norm_now = norm_next
        u_prev = u_now
        u_now = guess
    stress = stresses(carry, faces(u_now))
    fields = jnp.concatenate([u_now, stress], axis=0)
    table_x = block_table(fields.shape[1])
    table_y = block_table(fields.shape[2])
    table_z = block_table(fields.shape[3])
    blockc = jnp.einsum("ax,hxyz->hayz", table_x, fields, precision=lax.Precision.HIGHEST)
    blockc = jnp.einsum("by,hxyz->hxbz", table_y, blockc, precision=lax.Precision.HIGHEST)
    blockc = jnp.einsum("hxyz,cz->hxyc", blockc, table_z, precision=lax.Precision.HIGHEST)
    moved = jnp.transpose(blockc, (0, 2, 3, 1))
    shipped = lax.all_to_all(moved, "slab", split_axis=2, concat_axis=3, tiled=True)
    coeffs = wavelet(shipped)
    return (u_now, coeffs)


MESH = pl.DeviceIdType.MESH
HALO = 4
REACH = 3
SHEAR_REST = SPRING_NORMAL - SPRING_SHEAR


def wavelet_table(count):
    table = np.kron(np.eye(count // 4), cosine_table())
    pieces = []
    approx = table
    for level_index in range(LEVELS):
        even, odd = approx[0::2], approx[1::2]
        detail = odd - 0.5 * (even + np.roll(even, -1, axis=0))
        approx = even + 0.25 * (np.roll(detail, 1, axis=0) + detail)
        pieces.insert(0, detail)
    return np.concatenate([approx] + pieces, axis=0)


def split_table(table):
    high = table.astype(jnp.bfloat16).astype(np.float64)
    return high, (table - high).astype(jnp.bfloat16).astype(np.float64)


def sub_index():
    return lax.broadcasted_iota(jnp.int32, (8, 128), 0)


def lane_index():
    return lax.broadcasted_iota(jnp.int32, (8, 128), 1)


def up_y(a, b):
    ra, rb = pltpu.roll(a, 7, 0), pltpu.roll(b, 7, 0)
    last = sub_index() == 7
    return jnp.where(last, rb, ra), jnp.where(last, ra, rb)


def down_y(a, b):
    ra, rb = pltpu.roll(a, 1, 0), pltpu.roll(b, 1, 0)
    first = sub_index() == 0
    return jnp.where(first, rb, ra), jnp.where(first, ra, rb)


def up_z(v):
    return pltpu.roll(v, 127, 1)


def down_z(v):
    return pltpu.roll(v, 1, 1)


def total(v):
    return jnp.sum(jnp.sum(v, axis=0, keepdims=True), axis=1, keepdims=True)


def kernel(ns, ng, u_in, p_in, f_in, k_in, br_in, fl_in, ez_in, cz_in, gt_in,
           disp_out, coef_out,
           disp_ref, coef_ref, osem, u_ref, p_ref, f_ref, k_ref, br_ref, fl_ref, ez_ref, cz_ref, gt_ref, isem,
           e1a, e1b, s1, h1, e2a, e2b, s2, h2, rqa, rqb, e3a, s3, h3,
           u1a, u1b, carry, dga, dgb, kca, kcb, gath, rows, outb, inb,
           ctake, cland, csend, crecv, send4, recv4, send0, recv0, send1, recv1, send2, recv2, send3, recv3, asend, arecv, tsend, trecv):
    X, Y = u_ref.shape[1], u_ref.shape[2]
    si, gi = lax.axis_index("slab"), lax.axis_index("grp")
    me = si * ng + gi
    count = ns * ng
    fetched = []
    for at, (source, target) in enumerate((
        (br_in, br_ref), (fl_in, fl_ref), (ez_in, ez_ref), (k_in, k_ref), (u_in, u_ref), (p_in, p_ref),
        (f_in, f_ref), (cz_in, cz_ref), (gt_in, gt_ref),
    )):
        fetch = pltpu.make_async_copy(source, target, isem.at[at])
        fetch.start()
        fetched.append(fetch)
    barrier = pltpu.get_barrier_semaphore()

    others = []
    for k in sorted(range(ns), key=lambda k: -min(k, ns - k)):
        for g in range(ng):
            if k or g:
                others.append((lax.rem(si + k, ns), lax.rem(gi + g, ng)))
    for other in others:
        pl.semaphore_signal(barrier, inc=1, device_id=other, device_id_type=MESH)

    sub, lane = sub_index(), lane_index()
    upper = sub < 4

    steps = [(-1, 0), (1, 0), (0, -1), (0, 1), (-1, -1), (-1, 1), (1, -1), (1, 1)]

    def inside(ds, dg):
        ok = None
        if ds:
            ok = (si >= 1) if ds < 0 else (si <= ns - 2)
        if dg:
            more = (gi >= 1) if dg < 0 else (gi <= ng - 2)
            ok = more if ok is None else jnp.logical_and(ok, more)
        return ok

    def copies(ea, dst_a, stage, land, send, recv, low=0, high=None, ways=8, reach=REACH):
        half = X // 2
        edge = HALO // 2
        made = []
        chans = pl.ds(low, (ea.shape[0] if high is None else high) - low)
        for at, (ds, dg) in enumerate(steps[:ways]):
            if dg == 0:
                if ds < 0:
                    source = ea.at[chans, pl.ds(HALO, reach)]
                    target = dst_a.at[chans, pl.ds(HALO + X, reach)]
                else:
                    source = ea.at[chans, pl.ds(HALO + X - reach, reach)]
                    target = dst_a.at[chans, pl.ds(HALO - reach, reach)]
            else:
                side = 0 if dg < 0 else 1
                if ds == 0:
                    source, target = stage.at[side, chans], land.at[side, chans, pl.ds(edge, half)]
                elif ds < 0:
                    source = stage.at[side, chans, pl.ds(0, 1)]
                    target = land.at[side, chans, pl.ds(edge + half, 1)]
                else:
                    source = stage.at[side, chans, pl.ds(half - 1, 1)]
                    target = land.at[side, chans, pl.ds(edge - 1, 1)]
            made.append((ds, dg, pltpu.make_async_remote_copy(
                src_ref=source, dst_ref=target, send_sem=send.at[at], recv_sem=recv.at[at ^ 1 if at < 4 else 11 - at],
                device_id=(si + ds, gi + dg), device_id_type=MESH)))
        return made

    def begin(made):
        for ds, dg, copy in made:
            @pl.when(inside(ds, dg))
            def _():
                copy.start()

    def finish_recv(made, recv):
        for at, (ds, dg) in enumerate(steps[:len(made)]):
            back = made[at ^ 1 if at < 4 else 11 - at][2]

            @pl.when(inside(ds, dg))
            def _():
                back.wait_recv()

    def finish_send(made):
        for ds, dg, copy in made:
            @pl.when(inside(ds, dg))
            def _():
                copy.wait_send()

    def blank(dst_a, land):
        zero_a = jnp.zeros((dst_a.shape[0], HALO) + dst_a.shape[2:], jnp.float32)
        half, edge = X // 2, HALO // 2
        zero_l = jnp.zeros((land.shape[1], edge, 8, 128), jnp.float32)

        @pl.when(si == 0)
        def _():
            dst_a[:, pl.ds(0, HALO)] = zero_a
            for side in range(2):
                land[side, :, pl.ds(0, edge)] = zero_l

        @pl.when(si == ns - 1)
        def _():
            dst_a[:, pl.ds(HALO + X, HALO)] = zero_a
            for side in range(2):
                land[side, :, pl.ds(edge + half, edge)] = zero_l

        for side, edge_here in ((0, gi == ng - 1), (1, gi == 0)):
            @pl.when(edge_here)
            def _(side=side):
                land[side] = jnp.zeros(land.shape[1:], jnp.float32)

    def pack(stage, ch, pair, even, odd):
        stage[0, ch, pair] = jnp.where(upper, even, pltpu.roll(odd, 4, 0))
        stage[1, ch, pair] = jnp.where(upper, pltpu.roll(even, 4, 0), odd)

    def unpack(land, ch, pair):
        high, low = land[0, ch, pair], land[1, ch, pair]
        return (jnp.where(upper, high, pltpu.roll(low, 4, 0)),
                jnp.where(upper, pltpu.roll(high, 4, 0), low))

    def spread_rows(mask):
        wide = jnp.dot(mask.astype(jnp.float32), ez_ref[...], preferred_element_type=jnp.float32)
        return jnp.where(upper, jnp.broadcast_to(wide[0:1], (8, 128)), jnp.broadcast_to(wide[1:2], (8, 128)))

    for at in range(4):
        fetched[at].wait()
    for bx in range(X // 4):
        cut = 1.0 - CRACK_CUT * spread_rows(br_ref[bx])
        flag = spread_rows(fl_ref[bx])
        for at in range(4):
            x = bx * 4 + at
            w = k_ref[x] * cut
            e1a[6, HALO + x] = w
            carry[x] = flag * w

    def own(i, _):
        for c in range(3):
            tiles = []
            for o in range(2):
                x = 2 * i + o
                u = u_ref[c, x]
                f = f_ref[c, x]
                rhs = MASS_TERM * (2.0 * u - p_ref[c, x]) + f
                e1a[c, HALO + x] = u
                e1a[3 + c, HALO + x] = rhs
                e2a[c, HALO + x] = f
                tiles.append((u, rhs, f))
            pack(s1, c, i, tiles[0][0], tiles[1][0])
            pack(s1, 3 + c, i, tiles[0][1], tiles[1][1])
            pack(s2, c, i, tiles[0][2], tiles[1][2])
        pack(s1, 6, i, e1a[6, HALO + 2 * i], e1a[6, HALO + 2 * i + 1])
        return 0

    for at in range(4, 7):
        fetched[at].wait()
    lax.fori_loop(0, X // 2, own, 0)
    blank(e1a, h1)
    blank(e2a, h2)
    blank(e3a, h3)

    def corner_copies():
        made = []
        for at, (ds, dg) in enumerate(steps[4:]):
            side, end = (0 if dg < 0 else 1), (0 if ds < 0 else 1)
            made.append((ds, dg, pltpu.make_async_remote_copy(
                src_ref=ctake.at[side, end], dst_ref=cland.at[side, 1 - end],
                send_sem=csend.at[at], recv_sem=crecv.at[3 - at],
                device_id=(si + ds, gi + dg), device_id_type=MESH)))
        return made

    near = sub % 4 < 2
    for side in range(2):
        for end in range(2):
            for t in range((7 + 1) // 2):
                tile = s1[side, 2 * t, end * (X // 2 - 1)]
                if 2 * t + 1 < 7:
                    other = s1[side, 2 * t + 1, end * (X // 2 - 1)]
                    tile = (jnp.where(near, tile, pltpu.roll(other, 2, 0)) if side == 0
                            else jnp.where(near, pltpu.roll(other, 6, 0), tile))
                ctake[side, end, t] = tile

    def corner_unpack(made):
        for at, (ds, dg) in enumerate(steps[4:]):
            side, end = (0 if dg > 0 else 1), (1 if ds > 0 else 0)
            pair = HALO // 2 + X // 2 if ds > 0 else HALO // 2 - 1
            back = made[3 - at][2]

            @pl.when(inside(ds, dg))
            def _():
                back.wait_recv()
                for ch in range(7):
                    tile = cland[side, end, ch // 2]
                    h1[side, ch, pair] = tile if ch % 2 == 0 else pltpu.roll(tile, 6 if side == 0 else 2, 0)

    corners = corner_copies()
    zeroth = copies(e1a, e1a, s1, h1, send0, recv0, 6, 7, 4)
    first = copies(e1a, e1a, s1, h1, send1, recv1, 0, 3, 4)
    rest = copies(e1a, e1a, s1, h1, send4, recv4, 3, 6, 4, REACH - 1)
    second = copies(e2a, e2a, s2, h2, send2, recv2)
    third = copies(rqa, e3a, s3, h3, send3, recv3)
    pl.semaphore_wait(barrier, count - 1)
    begin(zeroth)
    begin(corners)
    begin(first)
    begin(rest)
    finish_recv(zeroth, recv0)
    corner_unpack(corners)

    def open0(i, _):
        e1b[6, 2 * i], e1b[6, 2 * i + 1] = unpack(h1, 6, i)
        return 0

    def open1(i, _):
        for ch in range(6):
            e1b[ch, 2 * i], e1b[ch, 2 * i + 1] = unpack(h1, ch, i)
        return 0

    lax.fori_loop(0, (X + 2 * HALO) // 2, open0, 0)

    def link(w, other):
        return jnp.where(jnp.minimum(w, other) > 0.0, 0.5 * (w + other), 0.0)

    not_last, not_first = lane < 127, lane > 0

    def coefficients(x, _):
        wa, wb = e1a[6, x], e1b[6, x]
        ya, yb = up_y(wa, wb)
        da, db = down_y(wa, wb)
        for w, wu, wd, yu, yd, dg, kc in (
            (wa, e1a[6, x + 1], e1a[6, x - 1], ya, da, dga, kca),
            (wb, e1b[6, x + 1], e1b[6, x - 1], yb, db, dgb, kcb),
        ):
            zu = jnp.where(not_last, up_z(w), 0.0)
            zd = jnp.where(not_first, down_z(w), 0.0)
            kc[0, x] = link(w, wu)
            kc[1, x] = link(w, yu)
            kc[2, x] = link(w, yd)
            kc[3, x] = link(w, zu)
            kc[4, x] = link(w, zd)
            sx = w + 0.5 * (wu + wd)
            sy = w + 0.5 * (yu + yd)
            sz = w + 0.5 * (zu + zd)
            every = MASS_TERM + SPRING_SHEAR * (sx + sy + sz)
            dg[0, x] = every + SHEAR_REST * sx
            dg[1, x] = every + SHEAR_REST * sy
            dg[2, x] = every + SHEAR_REST * sz
        return 0

    kca[0, HALO - REACH] = link(e1a[6, HALO - REACH], e1a[6, HALO - REACH + 1])
    kcb[0, HALO - REACH] = link(e1b[6, HALO - REACH], e1b[6, HALO - REACH + 1])
    lax.fori_loop(HALO - 2, HALO + X + 2, coefficients, 0)
    finish_recv(first, recv1)
    finish_recv(rest, recv4)
    begin(second)
    lax.fori_loop(0, (X + 2 * HALO) // 2, open1, 0)

    def operate(x, va, vb, base, both=True):
        result = []
        coef = [[kc[j, x] for j in range(5)] + [kc[0, x - 1]] for kc in (kca, kcb)]
        for c in range(3):
            a, b = va[base + c, x], vb[base + c, x]
            ua, ub = up_y(a, b)
            la, lb = down_y(a, b)
            pair = []
            halves = ((a, va, ua, la, coef[0], dga), (b, vb, ub, lb, coef[1], dgb))
            for v, ref, u, l, k, dg in halves if both else halves[:1]:
                parts = (
                    k[0] * ref[base + c, x + 1] + k[5] * ref[base + c, x - 1],
                    k[1] * u + k[2] * l,
                    k[3] * up_z(v) + k[4] * down_z(v),
                )
                every = parts[0] + parts[1] + parts[2]
                pair.append(dg[c, x] * v - (SPRING_SHEAR * every + SHEAR_REST * parts[c]))
            result.append(pair)
        return result

    def solve(step, va, vb, rhs_of):
        def residual(i, _):
            done = []
            for x in (2 * i, 2 * i + 1):
                image = operate(x, va, vb, 0)
                for c in range(3):
                    ra, rb = rhs_of(c, x)
                    done.append((c, x, ra - image[c][0], rb - image[c][1]))
            for c, x, ra, rb in done:
                rqa[c, x] = ra
                rqb[c, x] = rb
            return 0

        lax.fori_loop((HALO - 2) // 2, (HALO + X + 2) // 2, residual, 0)

        def put(x, image):
            for c in range(3):
                rqa[3 + c, x] = image[c][0]
                rqb[3 + c, x] = image[c][1]

        def apply(i, sums):
            rr, rq = sums
            at = (2 * i, 2 * i + 1)
            images = [operate(x, rqa, rqb, 0) for x in at]
            for x, image in zip(at, images):
                for c in range(3):
                    r = rqa[c, x]
                    rr, rq = rr + r * r, rq + r * image[c][0]
            for x, image in zip(at, images):
                put(x, image)
            return rr, rq

        zero = jnp.zeros((8, 128), jnp.float32)
        images = [operate(x, rqa, rqb, 0) for x in (HALO - 1, HALO + X)]
        put(HALO - 1, images[0])
        put(HALO + X, images[1])
        rr, rq = lax.fori_loop(HALO // 2, (HALO + X) // 2, apply, (zero, zero))
        rr, rq = total(rr), total(rq)
        mu = jnp.where(rr > 0.0, rq / jnp.where(rr > 0.0, rr, 1.0), 0.0)

        def centred(i, sums):
            ww, wr, mix, wt = sums
            for x in (2 * i, 2 * i + 1):
                image = operate(x, rqa, rqb, 3, False)
                for c in range(3):
                    r, q, s = rqa[c, x], rqa[3 + c, x], image[c][0]
                    w, t = q - mu * r, s - mu * q
                    ww, wr, mix, wt = ww + w * w, wr + w * r, mix + (r * t + w * q), wt + w * t
            return ww, wr, mix, wt

        sums = lax.fori_loop(HALO // 2, (HALO + X) // 2, centred, (zero,) * 4)
        ww, wr, mix, wt = [total(v) for v in sums]
        one = lax.broadcasted_iota(jnp.int32, (1, 128), 1)
        row = jnp.zeros((1, 128), jnp.float32)
        for at, value in enumerate((rr, rq, mu, ww, wr, mix, wt)):
            row = jnp.where(one == at, value, row)
        gath[step, me] = row

        for other in others:
            pltpu.make_async_remote_copy(
                src_ref=gath.at[step, me], dst_ref=gath.at[step, me], send_sem=asend.at[step], recv_sem=arecv.at[step],
                device_id=other, device_id_type=MESH).start()

    def collect(step):
        block = gath.at[step, pl.ds(0, count - 1)]
        pltpu.make_async_copy(block, block, arecv.at[step]).wait()
        table = gath[step].reshape(count, 128)
        rr, rq, mu, ww, wr, mix, wt = [table[:, at:at + 1] for at in range(7)]

        def down(v):
            return jnp.sum(v, axis=0, keepdims=True)

        norm = down(rr)
        alpha = norm / down(rq)
        rest = 1.0 - alpha * mu
        after = down(alpha * alpha * ww - 2.0 * alpha * rest * wr + rest * rest * rr)
        curved = down(rest * rest * rq - alpha * rest * mix + alpha * alpha * wt)
        ratio = after / norm
        beta = after / (curved - ratio * after / alpha)
        return alpha + beta * (1.0 + ratio), -beta * alpha

    def drain(step):
        block = gath.at[step, pl.ds(0, count - 1)]
        pltpu.make_async_copy(block, block, asend.at[step]).wait()

    solve(0, e1a, e1b, lambda c, x: (e1a[3 + c, x], e1b[3 + c, x]))

    def pack3(i, _):
        for ch in range(6):
            pack(s3, ch, i, rqa[ch, HALO + 2 * i], rqa[ch, HALO + 2 * i + 1])
        return 0

    lax.fori_loop(0, X // 2, pack3, 0)
    begin(third)

    finish_recv(second, recv2)

    def open2(i, _):
        for ch in range(3):
            e2b[ch, 2 * i], e2b[ch, 2 * i + 1] = unpack(h2, ch, i)
        return 0

    lax.fori_loop(0, (X + 2 * HALO) // 2, open2, 0)
    finish_recv(third, recv3)
    c0, c1 = collect(0)

    def step_b(i, _):
        for c in range(3):
            r0, r1 = unpack(h3, c, i)
            q0, q1 = unpack(h3, 3 + c, i)
            u1b[c, 2 * i] = e1b[c, 2 * i] + (c0 * r0 + c1 * q0)
            u1b[c, 2 * i + 1] = e1b[c, 2 * i + 1] + (c0 * r1 + c1 * q1)
        return 0

    lax.fori_loop(0, (X + 2 * HALO) // 2, step_b, 0)

    def step_a(i, _):
        for x in (2 * i, 2 * i + 1):
            for c in range(3):
                u1a[c, x] = e1a[c, x] + (c0 * rqa[c, x] + c1 * rqa[3 + c, x])
        return 0

    lax.fori_loop(HALO // 2, (HALO + X) // 2, step_a, 0)
    for x in list(range(HALO - REACH, HALO)) + list(range(HALO + X, HALO + X + REACH)):
        for c in range(3):
            u1a[c, x] = e1a[c, x] + (c0 * e3a[c, x] + c1 * e3a[3 + c, x])
    finish_send(zeroth)
    finish_send(corners)
    finish_send(rest)
    finish_send(first)
    finish_send(second)
    finish_send(third)

    def rhs2(c, x):
        return (MASS_TERM * (2.0 * u1a[c, x] - e1a[c, x]) + e2a[c, x],
                MASS_TERM * (2.0 * u1b[c, x] - e1b[c, x]) + e2b[c, x])

    solve(1, u1a, u1b, rhs2)
    c0, c1 = collect(1)

    def step2(x, _):
        for c in range(3):
            va = u1a[c, x] + (c0 * rqa[c, x] + c1 * rqa[3 + c, x])
            vb = u1b[c, x] + (c0 * rqb[c, x] + c1 * rqb[3 + c, x])
            u1a[c, x] = va
            u1b[c, x] = vb
        return 0

    step2(HALO - 1, 0)
    step2(HALO + X, 0)

    def step2_own(i, _):
        for x in (2 * i, 2 * i + 1):
            step2(x, 0)
            for c in range(3):
                v = u1a[c, x]
                disp_ref[c, x - HALO] = v
                rows[c, pl.ds(x - HALO, 8, stride=X), :] = v
        return 0

    lax.fori_loop(HALO // 2, (HALO + X) // 2, step2_own, 0)
    outputs = [pltpu.make_async_copy(disp_ref, disp_out, osem.at[6])]
    outputs += [pltpu.make_async_copy(coef_ref.at[c], coef_out.at[c], osem.at[c]) for c in range(6)]
    zrows = coef_ref.shape[2]
    nt = (((1,), (1,)), ((), ()))

    def halves(v):
        high = v.astype(jnp.bfloat16)
        return high, (v - high.astype(jnp.float32)).astype(jnp.bfloat16)

    def transform(c, _):
        high, low = halves(rows[c])
        turned = lax.dot_general(cz_ref[:, 0:256], jnp.concatenate([high, low], axis=1), nt,
                                 preferred_element_type=jnp.float32)
        turned += lax.dot_general(cz_ref[:, 256:384], high, nt, preferred_element_type=jnp.float32)
        for j in range(ns):
            outb[j, c] = turned[j * zrows:(j + 1) * zrows]
        return 0

    def trade(part, i):
        to = lax.rem(si + i, ns)
        return pltpu.make_async_remote_copy(
            src_ref=outb.at[to, pl.ds(3 * part, 3)], dst_ref=inb.at[si, pl.ds(3 * part, 3)],
            send_sem=tsend.at[part, i], recv_sem=trecv.at[part, i],
            device_id=(to, gi), device_id_type=MESH)

    trades = [[trade(part, i) for i in range(1, ns)] for part in range(2)]

    def ship(part):
        lax.fori_loop(3 * part, 3 * part + 3, transform, 0)
        for copy in trades[part]:
            copy.start()
        for c in range(3 * part, 3 * part + 3):
            inb[si, c] = outb[si, c]

    fetched[7].wait()
    ship(0)
    outputs[0].start()

    def finals(i, _):
        for x in (2 * i, 2 * i + 1):
            at = x - HALO
            scale = SPRING_NORMAL * carry[at] * 0.5
            a1, a2, b1 = u1a[1, x], u1a[2, x], u1b[1, x]
            dx = u1a[0, x + 1] - u1a[0, x - 1]
            dy = up_y(a1, b1)[0] - down_y(a1, b1)[0]
            dz = jnp.where(not_last, up_z(a2), 0.0) - jnp.where(not_first, down_z(a2), 0.0)
            for c, d in enumerate((dx, dy, dz)):
                rows[3 + c, pl.ds(at, 8, stride=X), :] = scale * d
        return 0

    lax.fori_loop(HALO // 2, (HALO + X) // 2, finals, 0)
    ship(1)
    fetched[8].wait()

    zlane = lax.broadcasted_iota(jnp.int32, (zrows, 128), 1)
    c1t, c3t = float(np.sqrt(0.5) * np.cos(np.pi / 8)), float(np.sqrt(0.5) * np.cos(3 * np.pi / 8))

    def gather_back(c, _):
        pieces = [inb[j, c] for j in range(ns)]
        gap = ns // 2
        while gap:
            keep = (zlane // (X * gap)) % 2 == 0
            mixed = list(pieces)
            for j in range(ns):
                if (j // gap) % 2 == 0:
                    a, b = pieces[j], pieces[j + gap]
                    mixed[j] = jnp.where(keep, a, pltpu.roll(b, X * gap, 1))
                    mixed[j + gap] = jnp.where(keep, pltpu.roll(a, 128 - X * gap, 1), b)
            pieces = mixed
            gap //= 2
        coded = []
        for b in range(Y // 4):
            v0, v1, v2, v3 = pieces[4 * b:4 * b + 4]
            s03, s12, d03, d12 = v0 + v3, v1 + v2, v0 - v3, v1 - v2
            coded += [0.5 * (s03 + s12), c1t * d03 + c3t * d12, 0.5 * (s03 - s12), c3t * d03 - c1t * d12]
        high, low = halves(jnp.concatenate(coded, axis=0))
        done = jnp.dot(jnp.concatenate([high, low], axis=1), gt_ref[...], preferred_element_type=jnp.float32)
        coef_ref[c] = (done[:, 0:128] + done[:, 128:256]).reshape(Y, zrows, 128)
        return 0

    for part in range(2):
        for copy in trades[part]:
            copy.wait_recv()
        for c in range(3 * part, 3 * part + 3):
            gather_back(c, 0)
            outputs[1 + c].start()
    drain(0)
    drain(1)
    for part in range(2):
        for copy in trades[part]:
            copy.wait_send()
    for copy in outputs:
        copy.wait()


def fused(mesh, u_now, u_prev, force, stiffness, broken, flags):
    ns, ng = mesh.shape["slab"], mesh.shape["grp"]
    _, X, Y, Z = u_now.shape
    xe, pairs, half = X + 2 * HALO, X // 2 + HALO, X // 2
    zrows = Z // ns
    ez = jnp.asarray(np.kron(np.eye(Z // 4), np.ones((1, 4))), jnp.float32)
    czh, czl = split_table(np.kron(np.eye(Z // 4), cosine_table()))
    cz = jnp.asarray(np.concatenate([czh, czh, czl], axis=1), jnp.bfloat16)
    gth, gtl = split_table(wavelet_table(X * ns).T)
    gt = jnp.asarray(np.block([[gth, gtl], [gth, np.zeros_like(gtl)]]), jnp.bfloat16)

    def vm(*shape):
        return pltpu.VMEM(shape, jnp.float32)

    def ext(n):
        return vm(n, xe, Y, Z)

    def stage(n):
        return vm(2, n, half, Y, Z)

    def land(n):
        return vm(2, n, pairs, Y, Z)

    dma = pltpu.SemaphoreType.DMA
    return pl.pallas_call(
        lambda *refs: kernel(ns, ng, *refs),
        name="lattice",
        out_shape=(jax.ShapeDtypeStruct(u_now.shape, jnp.float32),
                   jax.ShapeDtypeStruct((6, Y, zrows, X * ns), jnp.float32)),
        in_specs=[pl.BlockSpec(memory_space=pltpu.MemorySpace.HBM)] * 9,
        out_specs=(pl.BlockSpec(memory_space=pltpu.MemorySpace.HBM),) * 2,
        scratch_shapes=[
            vm(*u_now.shape), vm(6, Y, zrows, X * ns), pltpu.SemaphoreType.DMA((7,)),
            vm(*u_now.shape), vm(*u_now.shape), vm(*u_now.shape), vm(*stiffness.shape),
            pltpu.VMEM(broken.shape, broken.dtype), pltpu.VMEM(flags.shape, flags.dtype),
            vm(*ez.shape), pltpu.VMEM(cz.shape, cz.dtype), pltpu.VMEM(gt.shape, gt.dtype), pltpu.SemaphoreType.DMA((9,)),
            ext(7), ext(7), stage(7), land(7),
            ext(3), ext(3), stage(3), land(3),
            ext(6), ext(6), ext(6), stage(6), land(6),
            ext(3), ext(3), vm(X, Y, Z), ext(3), ext(3), ext(5), ext(5),
            vm(2, ns * ng, 1, 128), vm(6, Y * X, Z), vm(ns, 6, zrows, 128), vm(ns, 6, zrows, 128),
            vm(2, 2, 4, Y, Z), vm(2, 2, 4, Y, Z), dma((4,)), dma((4,)), dma((8,)), dma((8,)),
            dma((8,)), dma((8,)), dma((8,)), dma((8,)), dma((8,)), dma((8,)), dma((8,)), dma((8,)),
            dma((2,)), dma((2,)), dma((2, ns)), dma((2, ns)),
        ],
        compiler_params=pltpu.CompilerParams(collective_id=0, has_side_effects=True, vmem_limit_bytes=60 << 20),
    )(u_now, u_prev, force, stiffness, broken, flags, ez, cz, gt)


def fits(mesh, shape):
    ns, ng = mesh.shape["slab"], mesh.shape["grp"]
    x, y, z = shape[1] // ns, shape[2] // ng, shape[3]
    return y == 8 and z == 128 and x * y == 128 and x * ns == 128 and z % (8 * ns) == 0


def entry(mesh, *args):
    ns, ng = mesh.shape["slab"], mesh.shape["grp"]
    _, x, y, z = args[0].shape
    if fits(mesh, (3, x * ns, y * ng, z)):
        return fused(mesh, *args)
    return body(*args)


def solution(mesh):
    return jax.shard_map(
        lambda *args: entry(mesh, *args),
        mesh=mesh,
        in_specs=(
            P(None, "slab", "grp", None),
            P(None, "slab", "grp", None),
            P(None, "slab", "grp", None),
            P("slab", "grp", None),
            P("slab", "grp", None),
            P("slab", "grp", None),
        ),
        out_specs=(P(None, "slab", "grp", None), P(None, "grp", "slab", None)),
        check_vma=False,
    )
```

profile of v0, /device:TPU:0, one launch (start us, length us, event | category | flops | bytes accessed | tf_op | source)
XLA Modules:
  0.0 45.8 jit_solution(3603124205972787257)
XLA Ops:
  0.6 42.7 %lattice.1 = (f32[3,16,8,128]{3,2,1,0:T(8,128)}, f32[6,8,16,128]{3,2,1,0:T(8,128)}) custom-call(f32[3,16,8,128]{3,2,1,0:T(8,128)} %refs_0_.1, f32[3,16,8,128]{3,2,1,0:T(8,128)} %refs_1_.1, f32[3,16,8,128]{3,2,1,0:T(8,128)} %refs_2_.1, f32[16,8,128]{2,1,0:T(8,128)} %refs_3_.1, s32[4,2,32]{2,1,0:T(2,128)} %refs_4_.1, s32[4,2,32]{2,1,0:T(2,128)} %refs_5_.1, ...), custom_call_target="tpu_custom_call" | custom-call | tf_op jit(solution)/shard_map/lattice/pallas_call | solution.py:769
  43.3 0.0 copy-start
  43.3 1.7 %copy.13 = f32[3,16,8,128]{3,2,1,0:T(8,128)} copy(f32[3,16,8,128]{3,2,1,0:T(8,128)} %get-tuple-element.4) | data formatting | bytes 393216
  45.0 0.0 copy-done
  45.0 0.7 %copy.14 = f32[6,8,16,128]{3,2,1,0:T(8,128)} copy(f32[6,8,16,128]{3,2,1,0:T(8,128)S(1)} %copy-done) | data formatting | bytes 786432
Async XLA Ops:
  43.3 1.7 %copy-start = (f32[6,8,16,128]{3,2,1,0:T(8,128)S(1)}, f32[6,8,16,128]{3,2,1,0:T(8,128)}, u32[]{:S(2)}) copy-start(f32[6,8,16,128]{3,2,1,0:T(8,128)} %get-tuple-element.5) | copy-start | bytes 1179652
where the time goes:
time: 45.9 us; the launch traced here: 45.8 us
  Pallas kernels  42.7 us (93%)
  local copies, waits for them, and re-layouts  2.42 us (5%)
  between operations  0.65 us (1%)
    pallas_call x1, Pallas kernels, fused(): pl.pallas_call(lambda *refs: kernel(ns, ng, *refs), name='lattice', out_s...  42.7 us
    unnamed x4, local copies, waits for them, and re-layouts  2.42 us

commit v1 on v0

--- a/solution.py
+++ b/solution.py
@@ -210,8 +210,8 @@
 
 
 def kernel(ns, ng, u_in, p_in, f_in, k_in, br_in, fl_in, ez_in, cz_in, gt_in,
-           disp_out, coef_out,
-           disp_ref, coef_ref, osem, u_ref, p_ref, f_ref, k_ref, br_ref, fl_ref, ez_ref, cz_ref, gt_ref, isem,
+           disp_ref, coef_ref,
+           u_ref, p_ref, f_ref, k_ref, br_ref, fl_ref, ez_ref, cz_ref, gt_ref, isem,
            e1a, e1b, s1, h1, e2a, e2b, s2, h2, rqa, rqb, e3a, s3, h3,
            u1a, u1b, carry, dga, dgb, kca, kcb, gath, rows, outb, inb,
            ctake, cland, csend, crecv, send4, recv4, send0, recv0, send1, recv1, send2, recv2, send3, recv3, asend, arecv, tsend, trecv):
@@ -647,8 +647,6 @@
         return 0
 
     lax.fori_loop(HALO // 2, (HALO + X) // 2, step2_own, 0)
-    outputs = [pltpu.make_async_copy(disp_ref, disp_out, osem.at[6])]
-    outputs += [pltpu.make_async_copy(coef_ref.at[c], coef_out.at[c], osem.at[c]) for c in range(6)]
     zrows = coef_ref.shape[2]
     nt = (((1,), (1,)), ((), ()))
 
@@ -683,7 +681,6 @@
 
     fetched[7].wait()
     ship(0)
-    outputs[0].start()
 
     def finals(i, _):
         for x in (2 * i, 2 * i + 1):
@@ -732,13 +729,18 @@
             copy.wait_recv()
         for c in range(3 * part, 3 * part + 3):
             gather_back(c, 0)
-            outputs[1 + c].start()
     drain(0)
     drain(1)
     for part in range(2):
         for copy in trades[part]:
             copy.wait_send()
-    for copy in outputs:
+
+
+def store(disp_in, coef_in, disp_out, coef_out, sems):
+    copies = [pltpu.make_async_copy(disp_in, disp_out, sems.at[0]), pltpu.make_async_copy(coef_in, coef_out, sems.at[1])]
+    for copy in copies:
+        copy.start()
+    for copy in copies:
         copy.wait()
 
 
@@ -766,15 +768,16 @@
         return vm(2, n, pairs, Y, Z)
 
     dma = pltpu.SemaphoreType.DMA
-    return pl.pallas_call(
+    shapes = (u_now.shape, (6, Y, zrows, X * ns))
+    operands = [pltpu.with_memory_space_constraint(v, pltpu.HBM)
+                for v in (u_now, u_prev, force, stiffness, broken, flags, ez, cz, gt)]
+    results = pl.pallas_call(
         lambda *refs: kernel(ns, ng, *refs),
         name="lattice",
-        out_shape=(jax.ShapeDtypeStruct(u_now.shape, jnp.float32),
-                   jax.ShapeDtypeStruct((6, Y, zrows, X * ns), jnp.float32)),
+        out_shape=tuple(vm(*shape) for shape in shapes),
         in_specs=[pl.BlockSpec(memory_space=pltpu.MemorySpace.HBM)] * 9,
-        out_specs=(pl.BlockSpec(memory_space=pltpu.MemorySpace.HBM),) * 2,
+        out_specs=(pl.BlockSpec(memory_space=pltpu.VMEM),) * 2,
         scratch_shapes=[
-            vm(*u_now.shape), vm(6, Y, zrows, X * ns), pltpu.SemaphoreType.DMA((7,)),
             vm(*u_now.shape), vm(*u_now.shape), vm(*u_now.shape), vm(*stiffness.shape),
             pltpu.VMEM(broken.shape, broken.dtype), pltpu.VMEM(flags.shape, flags.dtype),
             vm(*ez.shape), pltpu.VMEM(cz.shape, cz.dtype), pltpu.VMEM(gt.shape, gt.dtype), pltpu.SemaphoreType.DMA((9,)),
@@ -787,8 +790,17 @@
             dma((8,)), dma((8,)), dma((8,)), dma((8,)), dma((8,)), dma((8,)), dma((8,)), dma((8,)),
             dma((2,)), dma((2,)), dma((2, ns)), dma((2, ns)),
         ],
-        compiler_params=pltpu.CompilerParams(collective_id=0, has_side_effects=True, vmem_limit_bytes=60 << 20),
-    )(u_now, u_prev, force, stiffness, broken, flags, ez, cz, gt)
+        compiler_params=pltpu.CompilerParams(collective_id=0, has_side_effects=True, vmem_limit_bytes=24 << 20),
+    )(*operands)
+    return pl.pallas_call(
+        store,
+        name="store",
+        out_shape=tuple(jax.ShapeDtypeStruct(shape, jnp.float32) for shape in shapes),
+        in_specs=[pl.BlockSpec(memory_space=pltpu.VMEM)] * 2,
+        out_specs=(pl.BlockSpec(memory_space=pltpu.MemorySpace.HBM),) * 2,
+        scratch_shapes=[dma((2,))],
+        compiler_params=pltpu.CompilerParams(vmem_limit_bytes=1 << 20),
+    )(*[pltpu.with_memory_space_constraint(v, pltpu.VMEM) for v in results])
 
 
 def fits(mesh, shape):

time: 45.9 us -> 43.7 us (0.952)
  local copies, waits for them, and re-layouts: 2.42 us -> 0 us
    unnamed x4 -> x0, local copies, waits for them, and re-layouts: 2.42 us -> none
    pallas_call x0 -> x1, Pallas kernels: none -> 0.83 us  [fused(): pl.pallas_call(store, name='store', out_shape=tuple((jax.ShapeDtypeStruct...]
    pallas_call x1, Pallas kernels: 42.7 us -> 42 us  [fused(): pl.pallas_call(lambda *refs: kernel(ns, ng, *refs), name='lattice', out_s...]
where the time goes in v1:
time: 43.7 us; the launch traced here: 43.5 us
  Pallas kernels  42.8 us (98%)
  between operations  0.64 us (1%)
    pallas_call x1, Pallas kernels, fused(): pl.pallas_call(lambda *refs: kernel(ns, ng, *refs), name='lattice', out_s...  42 us

profile of v1, /device:TPU:0, one launch (start us, length us, event | category | flops | bytes accessed | tf_op | source)
XLA Modules:
  0.0 43.5 jit_solution(16028969776378748403)
XLA Ops:
  0.6 42.0 %lattice.1 = (f32[3,16,8,128]{3,2,1,0:T(8,128)S(1)}, f32[6,8,16,128]{3,2,1,0:T(8,128)S(1)}) custom-call(f32[3,16,8,128]{3,2,1,0:T(8,128)} %refs_0_.1, f32[3,16,8,128]{3,2,1,0:T(8,128)} %refs_1_.1, f32[3,16,8,128]{3,2,1,0:T(8,128)} %refs_2_.1, f32[16,8,128]{2,1,0:T(8,128)} %refs_3_.1, s32[4,2,32]{2,1,0:T(2,128)} %refs_4_.1, s32[4,2,32]{2,1,0:T(2,128)} %refs_5_.1, ...), custom_call_target="tpu_custom_call" | custom-call | tf_op jit(solution)/shard_map/lattice/pallas_call | solution.py:774
  42.7 0.8 %store.1 = (f32[3,16,8,128]{3,2,1,0:T(8,128)}, f32[6,8,16,128]{3,2,1,0:T(8,128)}) custom-call(f32[3,16,8,128]{3,2,1,0:T(8,128)S(1)} %get-tuple-element.4.disp_in, f32[6,8,16,128]{3,2,1,0:T(8,128)S(1)} %get-tuple-element.5.coef_in), custom_call_target="tpu_custom_call" | custom-call | tf_op jit(solution)/shard_map/store/pallas_call | solution.py:795

commit v2 on v1

--- a/solution.py
+++ b/solution.py
@@ -212,9 +212,9 @@
 def kernel(ns, ng, u_in, p_in, f_in, k_in, br_in, fl_in, ez_in, cz_in, gt_in,
            disp_ref, coef_ref,
            u_ref, p_ref, f_ref, k_ref, br_ref, fl_ref, ez_ref, cz_ref, gt_ref, isem,
-           e1a, e1b, s1, h1, e2a, e2b, s2, h2, rqa, rqb, e3a, s3, h3,
+           e1a, e1b, s1, h1, e2a, e2b, s2, h2, rqa, rqb, s3, h3, k3,
            u1a, u1b, carry, dga, dgb, kca, kcb, gath, rows, outb, inb,
-           ctake, cland, csend, crecv, send4, recv4, send0, recv0, send1, recv1, send2, recv2, send3, recv3, asend, arecv, tsend, trecv):
+           ctake, cland, csend, crecv, send4, recv4, send0, recv0, send1, recv1, send2, recv2, send3, recv3, sendq, recvq, sendk, recvk, asend, arecv, tsend, trecv):
     X, Y = u_ref.shape[1], u_ref.shape[2]
     si, gi = lax.axis_index("slab"), lax.axis_index("grp")
     me = si * ng + gi
@@ -251,7 +251,8 @@
             ok = more if ok is None else jnp.logical_and(ok, more)
         return ok
 
-    def copies(ea, dst_a, stage, land, send, recv, low=0, high=None, ways=8, reach=REACH):
+    def copies(ea, dst_a, stage, land, send, recv, low=0, high=None, ways=8, reach=REACH, depth=None):
+        depth = reach if depth is None else depth
         half = X // 2
         edge = HALO // 2
         made = []
@@ -259,11 +260,11 @@
         for at, (ds, dg) in enumerate(steps[:ways]):
             if dg == 0:
                 if ds < 0:
-                    source = ea.at[chans, pl.ds(HALO, reach)]
-                    target = dst_a.at[chans, pl.ds(HALO + X, reach)]
+                    source = ea.at[chans, pl.ds(HALO + depth - reach, reach)]
+                    target = dst_a.at[chans, pl.ds(HALO + X + depth - reach, reach)]
                 else:
-                    source = ea.at[chans, pl.ds(HALO + X - reach, reach)]
-                    target = dst_a.at[chans, pl.ds(HALO - reach, reach)]
+                    source = ea.at[chans, pl.ds(HALO + X - depth, reach)]
+                    target = dst_a.at[chans, pl.ds(HALO - depth, reach)]
             else:
                 side = 0 if dg < 0 else 1
                 if ds == 0:
@@ -368,7 +369,18 @@
     lax.fori_loop(0, X // 2, own, 0)
     blank(e1a, h1)
     blank(e2a, h2)
-    blank(e3a, h3)
+    blank(rqa, h3)
+
+    def wedge_copies():
+        made = []
+        for at, (ds, dg) in enumerate(steps[4:]):
+            side, end = (0 if dg < 0 else 1), (0 if ds < 0 else 1)
+            pair = HALO // 2 + X // 2 if ds < 0 else HALO // 2 - 1
+            made.append((ds, dg, pltpu.make_async_remote_copy(
+                src_ref=k3.at[side, end], dst_ref=h3.at[side, :, pl.ds(pair, 1)],
+                send_sem=sendk.at[at], recv_sem=recvk.at[3 - at],
+                device_id=(si + ds, gi + dg), device_id_type=MESH)))
+        return made
 
     def corner_copies():
         made = []
@@ -408,8 +420,10 @@
     zeroth = copies(e1a, e1a, s1, h1, send0, recv0, 6, 7, 4)
     first = copies(e1a, e1a, s1, h1, send1, recv1, 0, 3, 4)
     rest = copies(e1a, e1a, s1, h1, send4, recv4, 3, 6, 4, REACH - 1)
-    second = copies(e2a, e2a, s2, h2, send2, recv2)
-    third = copies(rqa, e3a, s3, h3, send3, recv3)
+    second = copies(e2a, e2a, s2, h2, send2, recv2, reach=REACH - 1)
+    third = copies(rqa, rqa, s3, h3, send3, recv3, 0, 3, 4, 1, REACH)
+    outer = copies(rqa, rqa, s3, h3, sendq, recvq, 3, 6, 2, REACH - 1, REACH)
+    wedges = wedge_copies()
     pl.semaphore_wait(barrier, count - 1)
     begin(zeroth)
     begin(corners)
@@ -486,7 +500,7 @@
             result.append(pair)
         return result
 
-    def solve(step, va, vb, rhs_of):
+    def solve(step, va, vb, rhs_of, ship_halo=None):
         def residual(i, _):
             done = []
             for x in (2 * i, 2 * i + 1):
@@ -523,6 +537,8 @@
         put(HALO - 1, images[0])
         put(HALO + X, images[1])
         rr, rq = lax.fori_loop(HALO // 2, (HALO + X) // 2, apply, (zero, zero))
+        if ship_halo is not None:
+            ship_halo()
         rr, rq = total(rr), total(rq)
         mu = jnp.where(rr > 0.0, rq / jnp.where(rr > 0.0, rr, 1.0), 0.0)
 
@@ -571,16 +587,33 @@
         block = gath.at[step, pl.ds(0, count - 1)]
         pltpu.make_async_copy(block, block, asend.at[step]).wait()
 
-    solve(0, e1a, e1b, lambda c, x: (e1a[3 + c, x], e1b[3 + c, x]))
-
-    def pack3(i, _):
-        for ch in range(6):
-            pack(s3, ch, i, rqa[ch, HALO + 2 * i], rqa[ch, HALO + 2 * i + 1])
-        return 0
-
-    lax.fori_loop(0, X // 2, pack3, 0)
-    begin(third)
-
+    def joined(c, x, near, far):
+        r, q = rqa[c, x], rqa[3 + c, x]
+        return jnp.where(sub == 3, pltpu.roll(r, near, 0), jnp.where(sub == 4, pltpu.roll(r, far, 0), q))
+
+    def split(c, x, tile, row, near, far):
+        r = rqb[c, x]
+        rqb[c, x] = jnp.where(sub == row, pltpu.roll(tile, near, 0), jnp.where(sub == 7 - row, pltpu.roll(tile, far, 0), r))
+        rqb[3 + c, x] = tile
+
+    def ship_halo():
+        def pack3(i, _):
+            x = HALO + 2 * i
+            for c in range(3):
+                pack(s3, c, i, joined(c, x, 1, 7), joined(c, x + 1, 1, 7))
+            return 0
+
+        lax.fori_loop(0, X // 2, pack3, 0)
+        for end, x in ((0, HALO), (1, HALO + X - 2)):
+            for c in range(3):
+                even, odd = [joined(c, x + o, 2, 6) if o == end else joined(c, x + o, 3, 5) for o in range(2)]
+                k3[0, end, c, 0] = jnp.where(upper, even, pltpu.roll(odd, 4, 0))
+                k3[1, end, c, 0] = jnp.where(upper, pltpu.roll(even, 4, 0), odd)
+        begin(third)
+        begin(wedges)
+        begin(outer)
+
+    solve(0, e1a, e1b, lambda c, x: (e1a[3 + c, x], e1b[3 + c, x]), ship_halo)
     finish_recv(second, recv2)
 
     def open2(i, _):
@@ -590,34 +623,52 @@
 
     lax.fori_loop(0, (X + 2 * HALO) // 2, open2, 0)
     finish_recv(third, recv3)
+    for at, (ds, dg) in enumerate(steps[4:]):
+        back = wedges[3 - at][2]
+
+        @pl.when(inside(ds, dg))
+        def _():
+            back.wait_recv()
+
+    def open3(i, _):
+        for c in range(3):
+            even, odd = unpack(h3, c, i)
+            split(c, 2 * i, even, 2, 7, 1)
+            split(c, 2 * i + 1, odd, 2, 7, 1)
+        return 0
+
+    lax.fori_loop(HALO // 2, (HALO + X) // 2, open3, 0)
+    for pair, one in ((HALO // 2 - 1, 1), ((HALO + X) // 2, 0)):
+        for c in range(3):
+            for o, tile in enumerate(unpack(h3, c, pair)):
+                if o == one:
+                    split(c, 2 * pair + o, tile, 1, 6, 2)
+                else:
+                    split(c, 2 * pair + o, tile, 0, 5, 3)
+    finish_recv(outer, recvq)
     c0, c1 = collect(0)
 
-    def step_b(i, _):
+    def step1(x, both=True):
         for c in range(3):
-            r0, r1 = unpack(h3, c, i)
-            q0, q1 = unpack(h3, 3 + c, i)
-            u1b[c, 2 * i] = e1b[c, 2 * i] + (c0 * r0 + c1 * q0)
-            u1b[c, 2 * i + 1] = e1b[c, 2 * i + 1] + (c0 * r1 + c1 * q1)
-        return 0
-
-    lax.fori_loop(0, (X + 2 * HALO) // 2, step_b, 0)
-
-    def step_a(i, _):
-        for x in (2 * i, 2 * i + 1):
-            for c in range(3):
-                u1a[c, x] = e1a[c, x] + (c0 * rqa[c, x] + c1 * rqa[3 + c, x])
-        return 0
-
-    lax.fori_loop(HALO // 2, (HALO + X) // 2, step_a, 0)
-    for x in list(range(HALO - REACH, HALO)) + list(range(HALO + X, HALO + X + REACH)):
-        for c in range(3):
-            u1a[c, x] = e1a[c, x] + (c0 * e3a[c, x] + c1 * e3a[3 + c, x])
+            u1a[c, x] = e1a[c, x] + (c0 * rqa[c, x] + c1 * rqa[3 + c, x])
+            u1b[c, x] = e1b[c, x] + (c0 * rqb[c, x] + c1 * rqb[3 + c, x]) if both else jnp.zeros((8, 128), jnp.float32)
+
+    def step1_pair(i, _):
+        step1(2 * i)
+        step1(2 * i + 1)
+        return 0
+
+    lax.fori_loop(HALO // 2 - 1, (HALO + X) // 2 + 1, step1_pair, 0)
+    step1(HALO - REACH, False)
+    step1(HALO + X + REACH - 1, False)
     finish_send(zeroth)
     finish_send(corners)
     finish_send(rest)
     finish_send(first)
     finish_send(second)
     finish_send(third)
+    finish_send(outer)
+    finish_send(wedges)
 
     def rhs2(c, x):
         return (MASS_TERM * (2.0 * u1a[c, x] - e1a[c, x]) + e2a[c, x],
@@ -783,11 +834,11 @@
             vm(*ez.shape), pltpu.VMEM(cz.shape, cz.dtype), pltpu.VMEM(gt.shape, gt.dtype), pltpu.SemaphoreType.DMA((9,)),
             ext(7), ext(7), stage(7), land(7),
             ext(3), ext(3), stage(3), land(3),
-            ext(6), ext(6), ext(6), stage(6), land(6),
+            ext(6), ext(6), stage(3), land(3), vm(2, 2, 3, 1, Y, Z),
             ext(3), ext(3), vm(X, Y, Z), ext(3), ext(3), ext(5), ext(5),
             vm(2, ns * ng, 1, 128), vm(6, Y * X, Z), vm(ns, 6, zrows, 128), vm(ns, 6, zrows, 128),
-            vm(2, 2, 4, Y, Z), vm(2, 2, 4, Y, Z), dma((4,)), dma((4,)), dma((8,)), dma((8,)),
-            dma((8,)), dma((8,)), dma((8,)), dma((8,)), dma((8,)), dma((8,)), dma((8,)), dma((8,)),
+            vm(2, 2, 4, Y, Z), vm(2, 2, 4, Y, Z), dma((4,)), dma((4,)), dma((4,)), dma((4,)),
+            dma((4,)), dma((4,)), dma((4,)), dma((4,)), dma((8,)), dma((8,)), dma((4,)), dma((4,)), dma((2,)), dma((2,)), dma((4,)), dma((4,)),
             dma((2,)), dma((2,)), dma((2, ns)), dma((2, ns)),
         ],
         compiler_params=pltpu.CompilerParams(collective_id=0, has_side_effects=True, vmem_limit_bytes=24 << 20),

time: 43.7 us -> 41.6 us (0.952)
  Pallas kernels: 42.8 us -> 40.7 us
    pallas_call x1, Pallas kernels: 42 us -> 39.9 us  [fused(): pl.pallas_call(lambda *refs: kernel(ns, ng, *refs), name='lattice', out_s...]
where the time goes in v2:
time: 41.6 us; the launch traced here: 41.4 us
  Pallas kernels  40.7 us (98%)
  between operations  0.64 us (2%)
    pallas_call x1, Pallas kernels, fused(): pl.pallas_call(lambda *refs: kernel(ns, ng, *refs), name='lattice', out_s...  39.9 us

profile of v2, /device:TPU:0, one launch (start us, length us, event | category | flops | bytes accessed | tf_op | source)
XLA Modules:
  0.0 41.4 jit_solution(2081518060609339588)
XLA Ops:
  0.6 39.9 %lattice.1 = (f32[3,16,8,128]{3,2,1,0:T(8,128)S(1)}, f32[6,8,16,128]{3,2,1,0:T(8,128)S(1)}) custom-call(f32[3,16,8,128]{3,2,1,0:T(8,128)} %refs_0_.1, f32[3,16,8,128]{3,2,1,0:T(8,128)} %refs_1_.1, f32[3,16,8,128]{3,2,1,0:T(8,128)} %refs_2_.1, f32[16,8,128]{2,1,0:T(8,128)} %refs_3_.1, s32[4,2,32]{2,1,0:T(2,128)} %refs_4_.1, s32[4,2,32]{2,1,0:T(2,128)} %refs_5_.1, ...), custom_call_target="tpu_custom_call" | custom-call | tf_op jit(solution)/shard_map/lattice/pallas_call | solution.py:825
  40.5 0.8 %store.1 = (f32[3,16,8,128]{3,2,1,0:T(8,128)}, f32[6,8,16,128]{3,2,1,0:T(8,128)}) custom-call(f32[3,16,8,128]{3,2,1,0:T(8,128)S(1)} %get-tuple-element.4.disp_in, f32[6,8,16,128]{3,2,1,0:T(8,128)S(1)} %get-tuple-element.5.coef_in), custom_call_target="tpu_custom_call" | custom-call | tf_op jit(solution)/shard_map/store/pallas_call | solution.py:846

commit v3 on v2

--- a/solution.py
+++ b/solution.py
@@ -209,20 +209,20 @@
     return jnp.sum(jnp.sum(v, axis=0, keepdims=True), axis=1, keepdims=True)
 
 
-def kernel(ns, ng, u_in, p_in, f_in, k_in, br_in, fl_in, ez_in, cz_in, gt_in,
+def kernel(ns, ng, u_in, p_in, f_in, k_in, br_in, fl_in, ez_in, gt_in,
            disp_ref, coef_ref,
-           u_ref, p_ref, f_ref, k_ref, br_ref, fl_ref, ez_ref, cz_ref, gt_ref, isem,
+           u_ref, p_ref, f_ref, k_ref, br_ref, fl_ref, ez_ref, gt_ref, isem,
            e1a, e1b, s1, h1, e2a, e2b, s2, h2, rqa, rqb, s3, h3, k3,
-           u1a, u1b, carry, dga, dgb, kca, kcb, gath, rows, outb, inb,
+           u1a, u1b, scale, dga, dgb, kca, kcb, gath, rows, outb, inb, outx, inx, work,
            ctake, cland, csend, crecv, send4, recv4, send0, recv0, send1, recv1, send2, recv2, send3, recv3, sendq, recvq, sendk, recvk, asend, arecv, tsend, trecv):
-    X, Y = u_ref.shape[1], u_ref.shape[2]
+    X, Y, Z = u_ref.shape[1:]
     si, gi = lax.axis_index("slab"), lax.axis_index("grp")
     me = si * ng + gi
     count = ns * ng
     fetched = []
     for at, (source, target) in enumerate((
         (br_in, br_ref), (fl_in, fl_ref), (ez_in, ez_ref), (k_in, k_ref), (u_in, u_ref), (p_in, p_ref),
-        (f_in, f_ref), (cz_in, cz_ref), (gt_in, gt_ref),
+        (f_in, f_ref), (gt_in, gt_ref),
     )):
         fetch = pltpu.make_async_copy(source, target, isem.at[at])
         fetch.start()
@@ -344,7 +344,7 @@
             x = bx * 4 + at
             w = k_ref[x] * cut
             e1a[6, HALO + x] = w
-            carry[x] = flag * w
+            rows[3, pl.ds(x, 8, stride=X), :] = (SPRING_NORMAL * 0.5) * (flag * w)
 
     def own(i, _):
         for c in range(3):
@@ -371,6 +371,40 @@
     blank(e2a, h2)
     blank(rqa, h3)
 
+    zrows = Z // ns
+
+    def turn_out(value, out):
+        turned = value.T
+        for j in range(ns):
+            out[j] = turned[j * zrows:(j + 1) * zrows]
+        return turned
+
+    def spread_out(source, target, at):
+        for i in range(1, ns):
+            to = lax.rem(si + i, ns)
+            pltpu.make_async_remote_copy(
+                src_ref=source.at[to], dst_ref=target.at[si], send_sem=tsend.at[at], recv_sem=trecv.at[at],
+                device_id=(to, gi), device_id_type=MESH).start()
+
+    def landed(target, sem):
+        block = target.at[pl.ds(0, ns - 1)]
+        pltpu.make_async_copy(block, block, sem).wait()
+
+    def regroup(pieces):
+        lanes = lax.broadcasted_iota(jnp.int32, pieces[0].shape, 1)
+        gap = ns // 2
+        while gap:
+            keep = (lanes // (X * gap)) % 2 == 0
+            mixed = list(pieces)
+            for j in range(ns):
+                if (j // gap) % 2 == 0:
+                    a, b = pieces[j], pieces[j + gap]
+                    mixed[j] = jnp.where(keep, a, pltpu.roll(b, X * gap, 1))
+                    mixed[j + gap] = jnp.where(keep, pltpu.roll(a, 128 - X * gap, 1), b)
+            pieces = mixed
+            gap //= 2
+        return pieces
+
     def wedge_copies():
         made = []
         for at, (ds, dg) in enumerate(steps[4:]):
@@ -429,6 +463,8 @@
     begin(corners)
     begin(first)
     begin(rest)
+    turn_out(rows[3], outb.at[3])
+    inb[3, si] = outb[3, si]
     finish_recv(zeroth, recv0)
     corner_unpack(corners)
 
@@ -478,6 +514,7 @@
     finish_recv(first, recv1)
     finish_recv(rest, recv4)
     begin(second)
+    spread_out(outb.at[3], inb.at[3], 3)
     lax.fori_loop(0, (X + 2 * HALO) // 2, open1, 0)
 
     def operate(x, va, vb, base, both=True):
@@ -675,116 +712,105 @@
                 MASS_TERM * (2.0 * u1b[c, x] - e1b[c, x]) + e2b[c, x])
 
     solve(1, u1a, u1b, rhs2)
+    landed(inb.at[3], trecv.at[3])
+    for y, piece in enumerate(regroup([inb[3, j] for j in range(ns)])):
+        scale[y] = piece
     c0, c1 = collect(1)
 
-    def step2(x, _):
-        for c in range(3):
-            va = u1a[c, x] + (c0 * rqa[c, x] + c1 * rqa[3 + c, x])
-            vb = u1b[c, x] + (c0 * rqb[c, x] + c1 * rqb[3 + c, x])
-            u1a[c, x] = va
-            u1b[c, x] = vb
-        return 0
-
-    step2(HALO - 1, 0)
-    step2(HALO + X, 0)
-
-    def step2_own(i, _):
-        for x in (2 * i, 2 * i + 1):
-            step2(x, 0)
-            for c in range(3):
-                v = u1a[c, x]
-                disp_ref[c, x - HALO] = v
-                rows[c, pl.ds(x - HALO, 8, stride=X), :] = v
-        return 0
-
-    lax.fori_loop(HALO // 2, (HALO + X) // 2, step2_own, 0)
-    zrows = coef_ref.shape[2]
-    nt = (((1,), (1,)), ((), ()))
+    def step2(ra, rb, c, x):
+        return ra[c, x] + (c0 * rb[c, x] + c1 * rb[3 + c, x])
 
     def halves(v):
         high = v.astype(jnp.bfloat16)
         return high, (v - high.astype(jnp.float32)).astype(jnp.bfloat16)
 
-    def transform(c, _):
-        high, low = halves(rows[c])
-        turned = lax.dot_general(cz_ref[:, 0:256], jnp.concatenate([high, low], axis=1), nt,
-                                 preferred_element_type=jnp.float32)
-        turned += lax.dot_general(cz_ref[:, 256:384], high, nt, preferred_element_type=jnp.float32)
+    def finish(c):
+        for x in range(X):
+            v = step2(u1a, rqa, c, HALO + x)
+            disp_ref[c, x] = v
+            rows[c, pl.ds(x, 8, stride=X), :] = v
+        turned = turn_out(rows[c], outb.at[c])
+        spread_out(outb.at[c], inb.at[c], c)
+        inb[c, si] = outb[c, si]
+        return turned
+
+    def finish_edges(turned):
+        for x in range(X):
+            rows[4, pl.ds(x, 8, stride=X), :] = step2(u1b, rqb, 1, HALO + x)
+        sides_y = rows[4].T
+        zero = jnp.zeros((8, 128), jnp.float32)
         for j in range(ns):
-            outb[j, c] = turned[j * zrows:(j + 1) * zrows]
-        return 0
-
-    def trade(part, i):
-        to = lax.rem(si + i, ns)
-        return pltpu.make_async_remote_copy(
-            src_ref=outb.at[to, pl.ds(3 * part, 3)], dst_ref=inb.at[si, pl.ds(3 * part, 3)],
-            send_sem=tsend.at[part, i], recv_sem=trecv.at[part, i],
-            device_id=(to, gi), device_id_type=MESH)
-
-    trades = [[trade(part, i) for i in range(1, ns)] for part in range(2)]
-
-    def ship(part):
-        lax.fori_loop(3 * part, 3 * part + 3, transform, 0)
-        for copy in trades[part]:
-            copy.start()
-        for c in range(3 * part, 3 * part + 3):
-            inb[si, c] = outb[si, c]
-
+            low, high = sides_y[zrows * j:zrows * j + 8], sides_y[zrows * j + 8:zrows * j + 16]
+            tile = jnp.where(lane < 32, pltpu.roll(low, 16, 1),
+                             jnp.where(lane < 64, pltpu.roll(pltpu.roll(low, 4, 0), 48, 1),
+                                       jnp.where(lane < 96, pltpu.roll(high, 80, 1),
+                                                 pltpu.roll(pltpu.roll(high, 4, 0), 112, 1))))
+            before = pltpu.roll(turned[zrows * j - 8:zrows * j], 5, 0) if j else zero
+            after = pltpu.roll(turned[zrows * (j + 1):zrows * (j + 1) + 8], 5, 0) if j + 1 < ns else zero
+            outx[j] = jnp.where(sub == 4, before, jnp.where(sub == 5, after, tile))
+        spread_out(outx, inx, 4)
+        inx[si] = outx[si]
+
+    finish_edges(finish(2))
+    finish(0)
+    finish(1)
     fetched[7].wait()
-    ship(0)
-
-    def finals(i, _):
-        for x in (2 * i, 2 * i + 1):
-            at = x - HALO
-            scale = SPRING_NORMAL * carry[at] * 0.5
-            a1, a2, b1 = u1a[1, x], u1a[2, x], u1b[1, x]
-            dx = u1a[0, x + 1] - u1a[0, x - 1]
-            dy = up_y(a1, b1)[0] - down_y(a1, b1)[0]
-            dz = jnp.where(not_last, up_z(a2), 0.0) - jnp.where(not_first, down_z(a2), 0.0)
-            for c, d in enumerate((dx, dy, dz)):
-                rows[3 + c, pl.ds(at, 8, stride=X), :] = scale * d
-        return 0
-
-    lax.fori_loop(HALO // 2, (HALO + X) // 2, finals, 0)
-    ship(1)
-    fetched[8].wait()
-
-    zlane = lax.broadcasted_iota(jnp.int32, (zrows, 128), 1)
+
     c1t, c3t = float(np.sqrt(0.5) * np.cos(np.pi / 8)), float(np.sqrt(0.5) * np.cos(3 * np.pi / 8))
 
-    def gather_back(c, _):
-        pieces = [inb[j, c] for j in range(ns)]
-        gap = ns // 2
-        while gap:
-            keep = (zlane // (X * gap)) % 2 == 0
-            mixed = list(pieces)
-            for j in range(ns):
-                if (j // gap) % 2 == 0:
-                    a, b = pieces[j], pieces[j + gap]
-                    mixed[j] = jnp.where(keep, a, pltpu.roll(b, X * gap, 1))
-                    mixed[j + gap] = jnp.where(keep, pltpu.roll(a, 128 - X * gap, 1), b)
-            pieces = mixed
-            gap //= 2
-        coded = []
+    def cosine(v0, v1, v2, v3):
+        s03, s12, d03, d12 = v0 + v3, v1 + v2, v0 - v3, v1 - v2
+        return [0.5 * (s03 + s12), c1t * d03 + c3t * d12, 0.5 * (s03 - s12), c3t * d03 - c1t * d12]
+
+    def encode(ch, fields):
         for b in range(Y // 4):
-            v0, v1, v2, v3 = pieces[4 * b:4 * b + 4]
-            s03, s12, d03, d12 = v0 + v3, v1 + v2, v0 - v3, v1 - v2
-            coded += [0.5 * (s03 + s12), c1t * d03 + c3t * d12, 0.5 * (s03 - s12), c3t * d03 - c1t * d12]
-        high, low = halves(jnp.concatenate(coded, axis=0))
+            for k, v in enumerate(cosine(*fields[4 * b:4 * b + 4])):
+                work[ch, (4 * b + k) * zrows:(4 * b + k + 1) * zrows] = v
+        parts = []
+        for p in range(Y * zrows // 32):
+            parts += cosine(*[work[ch, pl.ds(32 * p + n, 8, stride=4), :] for n in range(4)])
+        high, low = halves(jnp.concatenate(parts, axis=0))
         done = jnp.dot(jnp.concatenate([high, low], axis=1), gt_ref[...], preferred_element_type=jnp.float32)
-        coef_ref[c] = (done[:, 0:128] + done[:, 128:256]).reshape(Y, zrows, 128)
-        return 0
-
-    for part in range(2):
-        for copy in trades[part]:
-            copy.wait_recv()
-        for c in range(3 * part, 3 * part + 3):
-            gather_back(c, 0)
+        done = done[:, 0:128] + done[:, 128:256]
+        for p in range(Y * zrows // 32):
+            for n in range(4):
+                coef_ref[ch, pl.ds(32 * p + n, 8, stride=4), :] = done[(4 * p + n) * 8:(4 * p + n + 1) * 8]
+
+    def arrived(c):
+        landed(inb.at[c], trecv.at[c])
+        return regroup([inb[c, j] for j in range(ns)])
+
+    field = arrived(2)
+    encode(2, field)
+    landed(inx, trecv.at[4])
+    edges = regroup([inx[j] for j in range(ns)])
+    stress = []
+    for y in range(Y):
+        low, high = field[y][0:8], field[y][8:16]
+        ul, uh, dl, dh = pltpu.roll(low, 7, 0), pltpu.roll(high, 7, 0), pltpu.roll(low, 1, 0), pltpu.roll(high, 1, 0)
+        first, last = sub == 0, sub == 7
+        low = jnp.where(last, uh, ul) - jnp.where(first, pltpu.roll(edges[y], 4, 0), dl)
+        high = jnp.where(last, pltpu.roll(edges[y], 2, 0), uh) - jnp.where(first, dl, dh)
+        stress.append(scale[y] * jnp.concatenate([low, high], axis=0))
+    encode(5, stress)
+    field = arrived(0)
+    encode(0, field)
+    wide = lax.broadcasted_iota(jnp.int32, (zrows, 128), 1)
+    encode(3, [scale[y] * (jnp.where(wide < 127, up_z(field[y]), 0.0) - jnp.where(wide > 0, down_z(field[y]), 0.0))
+               for y in range(Y)])
+    field = arrived(1)
+    encode(1, field)
+    outside = []
+    for side in range(2):
+        quarter = [edges[2 * q + side] for q in range(4)]
+        outside.append(jnp.concatenate([jnp.where(upper, quarter[q], pltpu.roll(quarter[q + 1], 4, 0)) for q in (0, 2)], axis=0))
+    field = [outside[0]] + field + [outside[1]]
+    encode(4, [scale[y] * (field[y + 2] - field[y]) for y in range(Y)])
     drain(0)
     drain(1)
-    for part in range(2):
-        for copy in trades[part]:
-            copy.wait_send()
+    for at in range(4):
+        landed(inb.at[at], tsend.at[at])
+    landed(inx, tsend.at[4])
 
 
 def store(disp_in, coef_in, disp_out, coef_out, sems):
@@ -801,8 +827,6 @@
     xe, pairs, half = X + 2 * HALO, X // 2 + HALO, X // 2
     zrows = Z // ns
     ez = jnp.asarray(np.kron(np.eye(Z // 4), np.ones((1, 4))), jnp.float32)
-    czh, czl = split_table(np.kron(np.eye(Z // 4), cosine_table()))
-    cz = jnp.asarray(np.concatenate([czh, czh, czl], axis=1), jnp.bfloat16)
     gth, gtl = split_table(wavelet_table(X * ns).T)
     gt = jnp.asarray(np.block([[gth, gtl], [gth, np.zeros_like(gtl)]]), jnp.bfloat16)
 
@@ -819,31 +843,31 @@
         return vm(2, n, pairs, Y, Z)
 
     dma = pltpu.SemaphoreType.DMA
-    shapes = (u_now.shape, (6, Y, zrows, X * ns))
+    shapes = (u_now.shape, (6, Y * zrows, X * ns))
     operands = [pltpu.with_memory_space_constraint(v, pltpu.HBM)
-                for v in (u_now, u_prev, force, stiffness, broken, flags, ez, cz, gt)]
+                for v in (u_now, u_prev, force, stiffness, broken, flags, ez, gt)]
     results = pl.pallas_call(
         lambda *refs: kernel(ns, ng, *refs),
         name="lattice",
         out_shape=tuple(vm(*shape) for shape in shapes),
-        in_specs=[pl.BlockSpec(memory_space=pltpu.MemorySpace.HBM)] * 9,
+        in_specs=[pl.BlockSpec(memory_space=pltpu.MemorySpace.HBM)] * 8,
         out_specs=(pl.BlockSpec(memory_space=pltpu.VMEM),) * 2,
         scratch_shapes=[
             vm(*u_now.shape), vm(*u_now.shape), vm(*u_now.shape), vm(*stiffness.shape),
             pltpu.VMEM(broken.shape, broken.dtype), pltpu.VMEM(flags.shape, flags.dtype),
-            vm(*ez.shape), pltpu.VMEM(cz.shape, cz.dtype), pltpu.VMEM(gt.shape, gt.dtype), pltpu.SemaphoreType.DMA((9,)),
+            vm(*ez.shape), pltpu.VMEM(gt.shape, gt.dtype), pltpu.SemaphoreType.DMA((8,)),
             ext(7), ext(7), stage(7), land(7),
             ext(3), ext(3), stage(3), land(3),
             ext(6), ext(6), stage(3), land(3), vm(2, 2, 3, 1, Y, Z),
-            ext(3), ext(3), vm(X, Y, Z), ext(3), ext(3), ext(5), ext(5),
-            vm(2, ns * ng, 1, 128), vm(6, Y * X, Z), vm(ns, 6, zrows, 128), vm(ns, 6, zrows, 128),
+            ext(3), ext(3), vm(Y, zrows, X * ns), ext(3), ext(3), ext(5), ext(5),
+            vm(2, ns * ng, 1, 128), vm(5, Y * X, Z), vm(4, ns, zrows, 128), vm(4, ns, zrows, 128), vm(ns, 8, 128), vm(ns, 8, 128), vm(6, Y * zrows, X * ns),
             vm(2, 2, 4, Y, Z), vm(2, 2, 4, Y, Z), dma((4,)), dma((4,)), dma((4,)), dma((4,)),
             dma((4,)), dma((4,)), dma((4,)), dma((4,)), dma((8,)), dma((8,)), dma((4,)), dma((4,)), dma((2,)), dma((2,)), dma((4,)), dma((4,)),
-            dma((2,)), dma((2,)), dma((2, ns)), dma((2, ns)),
+            dma((2,)), dma((2,)), dma((5,)), dma((5,)),
         ],
         compiler_params=pltpu.CompilerParams(collective_id=0, has_side_effects=True, vmem_limit_bytes=24 << 20),
     )(*operands)
-    return pl.pallas_call(
+    disp, coef = pl.pallas_call(
         store,
         name="store",
         out_shape=tuple(jax.ShapeDtypeStruct(shape, jnp.float32) for shape in shapes),
@@ -852,6 +876,7 @@
         scratch_shapes=[dma((2,))],
         compiler_params=pltpu.CompilerParams(vmem_limit_bytes=1 << 20),
     )(*[pltpu.with_memory_space_constraint(v, pltpu.VMEM) for v in results])
+    return disp, coef.reshape(6, Y, zrows, X * ns)
 
 
 def fits(mesh, shape):

time: 41.6 us -> 38.4 us (0.923)
  Pallas kernels: 40.7 us -> 37.5 us
    pallas_call x1, Pallas kernels: 39.9 us -> 36.7 us  [fused(): pl.pallas_call(lambda *refs: kernel(ns, ng, *refs), name='lattice', out_s...]
where the time goes in v3:
time: 38.4 us; the launch traced here: 38.2 us
  Pallas kernels  37.5 us (98%)
  between operations  0.64 us (2%)
    pallas_call x1, Pallas kernels, fused(): pl.pallas_call(lambda *refs: kernel(ns, ng, *refs), name='lattice', out_s...  36.7 us
    pallas_call x1, Pallas kernels, fused(): pl.pallas_call(store, name='store', out_shape=tuple((jax.ShapeDtypeStruct...  0.83 us

profile of v3, /device:TPU:0, one launch (start us, length us, event | category | flops | bytes accessed | tf_op | source)
XLA Modules:
  0.0 38.2 jit_solution(2737191526181695861)
XLA Ops:
  0.6 36.7 %lattice.1 = (f32[3,16,8,128]{3,2,1,0:T(8,128)S(1)}, f32[6,128,128]{2,1,0:T(8,128)S(1)}) custom-call(f32[3,16,8,128]{3,2,1,0:T(8,128)} %refs_0_.1, f32[3,16,8,128]{3,2,1,0:T(8,128)} %refs_1_.1, f32[3,16,8,128]{3,2,1,0:T(8,128)} %refs_2_.1, f32[16,8,128]{2,1,0:T(8,128)} %refs_3_.1, s32[4,2,32]{2,1,0:T(2,128)} %refs_4_.1, s32[4,2,32]{2,1,0:T(2,128)} %refs_5_.1, ...), custom_call_target="tpu_custom_call" | custom-call | tf_op jit(solution)/shard_map/lattice/pallas_call | solution.py:849
  37.3 0.8 %store.1 = (f32[3,16,8,128]{3,2,1,0:T(8,128)}, f32[6,128,128]{2,1,0:T(8,128)}) custom-call(f32[3,16,8,128]{3,2,1,0:T(8,128)S(1)} %get-tuple-element.6.disp_in, f32[6,128,128]{2,1,0:T(8,128)S(1)} %get-tuple-element.7.coef_in), custom_call_target="tpu_custom_call" | custom-call | tf_op jit(solution)/shard_map/store/pallas_call | solution.py:870

commit v4 on v3

--- a/solution.py
+++ b/solution.py
@@ -158,6 +158,7 @@
 HALO = 4
 REACH = 3
 SHEAR_REST = SPRING_NORMAL - SPRING_SHEAR
+WIDE_R, WIDE_A, WIDE_C, WIDE_K = 10, 8, 8, 10
 
 
 def wavelet_table(count):
@@ -480,11 +481,24 @@
     lax.fori_loop(0, (X + 2 * HALO) // 2, open0, 0)
 
     def link(w, other):
-        return jnp.where(jnp.minimum(w, other) > 0.0, 0.5 * (w + other), 0.0)
+        return jnp.where(jnp.minimum(w, other) > 0.0, (0.5 * SPRING_SHEAR) * (w + other), 0.0)
 
     not_last, not_first = lane < 127, lane > 0
 
-    def coefficients(x, _):
+    def over_rows(low, high, width, body, carried=0):
+        width = max(v for v in range(1, width + 1) if (high - low) % v == 0)
+
+        def chunk(i, state):
+            return body([low + i * width + o for o in range(width)], state)
+
+        return lax.fori_loop(0, (high - low) // width, chunk, carried)
+
+    def all_coefficients(rows_here, _):
+        for x in rows_here:
+            coefficients(x)
+        return 0
+
+    def coefficients(x):
         wa, wb = e1a[6, x], e1b[6, x]
         ya, yb = up_y(wa, wb)
         da, db = down_y(wa, wb)
@@ -506,11 +520,10 @@
             dg[0, x] = every + SHEAR_REST * sx
             dg[1, x] = every + SHEAR_REST * sy
             dg[2, x] = every + SHEAR_REST * sz
-        return 0
 
     kca[0, HALO - REACH] = link(e1a[6, HALO - REACH], e1a[6, HALO - REACH + 1])
     kcb[0, HALO - REACH] = link(e1b[6, HALO - REACH], e1b[6, HALO - REACH + 1])
-    lax.fori_loop(HALO - 2, HALO + X + 2, coefficients, 0)
+    over_rows(HALO - 2, HALO + X + 2, WIDE_K, all_coefficients)
     finish_recv(first, recv1)
     finish_recv(rest, recv4)
     begin(second)
@@ -532,40 +545,35 @@
                     k[1] * u + k[2] * l,
                     k[3] * up_z(v) + k[4] * down_z(v),
                 )
-                every = parts[0] + parts[1] + parts[2]
-                pair.append(dg[c, x] * v - (SPRING_SHEAR * every + SHEAR_REST * parts[c]))
+                shear = parts[(c + 1) % 3] + parts[(c + 2) % 3]
+                pair.append(dg[c, x] * v - (shear + (SPRING_NORMAL / SPRING_SHEAR) * parts[c]))
             result.append(pair)
         return result
 
     def solve(step, va, vb, rhs_of, ship_halo=None):
-        def residual(i, _):
-            done = []
-            for x in (2 * i, 2 * i + 1):
+        def residual(rows_here, _):
+            for x in rows_here:
                 image = operate(x, va, vb, 0)
                 for c in range(3):
                     ra, rb = rhs_of(c, x)
-                    done.append((c, x, ra - image[c][0], rb - image[c][1]))
-            for c, x, ra, rb in done:
-                rqa[c, x] = ra
-                rqb[c, x] = rb
+                    rqa[c, x] = ra - image[c][0]
+                    rqb[c, x] = rb - image[c][1]
             return 0
 
-        lax.fori_loop((HALO - 2) // 2, (HALO + X + 2) // 2, residual, 0)
+        over_rows(HALO - 2, HALO + X + 2, WIDE_R, residual)
 
         def put(x, image):
             for c in range(3):
                 rqa[3 + c, x] = image[c][0]
                 rqb[3 + c, x] = image[c][1]
 
-        def apply(i, sums):
+        def apply(rows_here, sums):
             rr, rq = sums
-            at = (2 * i, 2 * i + 1)
-            images = [operate(x, rqa, rqb, 0) for x in at]
-            for x, image in zip(at, images):
+            for x in rows_here:
+                image = operate(x, rqa, rqb, 0)
                 for c in range(3):
                     r = rqa[c, x]
                     rr, rq = rr + r * r, rq + r * image[c][0]
-            for x, image in zip(at, images):
                 put(x, image)
             return rr, rq
 
@@ -573,15 +581,15 @@
         images = [operate(x, rqa, rqb, 0) for x in (HALO - 1, HALO + X)]
         put(HALO - 1, images[0])
         put(HALO + X, images[1])
-        rr, rq = lax.fori_loop(HALO // 2, (HALO + X) // 2, apply, (zero, zero))
+        rr, rq = over_rows(HALO, HALO + X, WIDE_A, apply, (zero, zero))
         if ship_halo is not None:
             ship_halo()
         rr, rq = total(rr), total(rq)
         mu = jnp.where(rr > 0.0, rq / jnp.where(rr > 0.0, rr, 1.0), 0.0)
 
-        def centred(i, sums):
+        def centred(rows_here, sums):
             ww, wr, mix, wt = sums
-            for x in (2 * i, 2 * i + 1):
+            for x in rows_here:
                 image = operate(x, rqa, rqb, 3, False)
                 for c in range(3):
                     r, q, s = rqa[c, x], rqa[3 + c, x], image[c][0]
@@ -589,7 +597,7 @@
                     ww, wr, mix, wt = ww + w * w, wr + w * r, mix + (r * t + w * q), wt + w * t
             return ww, wr, mix, wt
 
-        sums = lax.fori_loop(HALO // 2, (HALO + X) // 2, centred, (zero,) * 4)
+        sums = over_rows(HALO, HALO + X, WIDE_C, centred, (zero,) * 4)
         ww, wr, mix, wt = [total(v) for v in sums]
         one = lax.broadcasted_iota(jnp.int32, (1, 128), 1)
         row = jnp.zeros((1, 128), jnp.float32)

time: 38.4 us -> 36.1 us (0.940)
  Pallas kernels: 37.5 us -> 35.3 us
    pallas_call x1, Pallas kernels: 36.7 us -> 34.5 us  [fused(): pl.pallas_call(lambda *refs: kernel(ns, ng, *refs), name='lattice', out_s...]
where the time goes in v4:
time: 36.1 us; the launch traced here: 36 us
  Pallas kernels  35.3 us (98%)
  between operations  0.64 us (2%)
    pallas_call x1, Pallas kernels, fused(): pl.pallas_call(lambda *refs: kernel(ns, ng, *refs), name='lattice', out_s...  34.5 us
    pallas_call x1, Pallas kernels, fused(): pl.pallas_call(store, name='store', out_shape=tuple((jax.ShapeDtypeStruct...  0.83 us

profile of v4, /device:TPU:0, one launch (start us, length us, event | category | flops | bytes accessed | tf_op | source)
XLA Modules:
  0.0 36.0 jit_solution(718892729424781646)
XLA Ops:
  0.6 34.5 %lattice.1 = (f32[3,16,8,128]{3,2,1,0:T(8,128)S(1)}, f32[6,128,128]{2,1,0:T(8,128)S(1)}) custom-call(f32[3,16,8,128]{3,2,1,0:T(8,128)} %refs_0_.1, f32[3,16,8,128]{3,2,1,0:T(8,128)} %refs_1_.1, f32[3,16,8,128]{3,2,1,0:T(8,128)} %refs_2_.1, f32[16,8,128]{2,1,0:T(8,128)} %refs_3_.1, s32[4,2,32]{2,1,0:T(2,128)} %refs_4_.1, s32[4,2,32]{2,1,0:T(2,128)} %refs_5_.1, ...), custom_call_target="tpu_custom_call" | custom-call | tf_op jit(solution)/shard_map/lattice/pallas_call | solution.py:857
  35.1 0.8 %store.1 = (f32[3,16,8,128]{3,2,1,0:T(8,128)}, f32[6,128,128]{2,1,0:T(8,128)}) custom-call(f32[3,16,8,128]{3,2,1,0:T(8,128)S(1)} %get-tuple-element.6.disp_in, f32[6,128,128]{2,1,0:T(8,128)S(1)} %get-tuple-element.7.coef_in), custom_call_target="tpu_custom_call" | custom-call | tf_op jit(solution)/shard_map/store/pallas_call | solution.py:878

commit v5 on v4

--- a/solution.py
+++ b/solution.py
@@ -158,7 +158,7 @@
 HALO = 4
 REACH = 3
 SHEAR_REST = SPRING_NORMAL - SPRING_SHEAR
-WIDE_R, WIDE_A, WIDE_C, WIDE_K = 10, 8, 8, 10
+WIDE_R, WIDE_A, WIDE_C, WIDE_K = 20, 16, 16, 20
 
 
 def wavelet_table(count):
@@ -214,12 +214,51 @@
            disp_ref, coef_ref,
            u_ref, p_ref, f_ref, k_ref, br_ref, fl_ref, ez_ref, gt_ref, isem,
            e1a, e1b, s1, h1, e2a, e2b, s2, h2, rqa, rqb, s3, h3, k3,
-           u1a, u1b, scale, dga, dgb, kca, kcb, gath, rows, outb, inb, outx, inx, work,
+           u1a, u1b, scale, dga, dgb, kca, kcb, known, gath, rows, outb, inb, outx, inx, work,
            ctake, cland, csend, crecv, send4, recv4, send0, recv0, send1, recv1, send2, recv2, send3, recv3, sendq, recvq, sendk, recvk, asend, arecv, tsend, trecv):
     X, Y, Z = u_ref.shape[1:]
     si, gi = lax.axis_index("slab"), lax.axis_index("grp")
     me = si * ng + gi
     count = ns * ng
+    barrier = pltpu.get_barrier_semaphore()
+
+    others = []
+    for k in sorted(range(ns), key=lambda k: -min(k, ns - k)):
+        for g in range(ng):
+            if k or g:
+                others.append((lax.rem(si + k, ns), lax.rem(gi + g, ng)))
+    sub, lane = sub_index(), lane_index()
+    upper = sub < 4
+
+    steps = [(-1, 0), (1, 0), (0, -1), (0, 1), (-1, -1), (-1, 1), (1, -1), (1, 1)]
+
+    def inside(ds, dg):
+        ok = None
+        if ds:
+            ok = (si >= -ds) if ds < 0 else (si <= ns - 1 - ds)
+        if dg:
+            more = (gi >= -dg) if dg < 0 else (gi <= ng - 1 - dg)
+            ok = more if ok is None else jnp.logical_and(ok, more)
+        return ok
+
+    def around(reach):
+        return [(ds, dg) for ds in (-reach, 0, reach) for dg in (-reach, 0, reach)
+                if (ds or dg) and abs(ds) < ns and abs(dg) < ng]
+
+    def greet(sem, reach):
+        for ds, dg in around(reach):
+            @pl.when(inside(ds, dg))
+            def _():
+                pl.semaphore_signal(sem, inc=1, device_id=(si + ds, gi + dg), device_id_type=MESH)
+
+    def meet(sem, reach):
+        pl.semaphore_wait(sem, sum(jnp.where(inside(ds, dg), 1, 0) for ds, dg in around(reach)))
+
+    rounds = []
+    while (rounds[-1] * 2 if rounds else 1) < max(ns, ng):
+        rounds.append(rounds[-1] * 2 if rounds else 1)
+
+    greet(barrier, 1)
     fetched = []
     for at, (source, target) in enumerate((
         (br_in, br_ref), (fl_in, fl_ref), (ez_in, ez_ref), (k_in, k_ref), (u_in, u_ref), (p_in, p_ref),
@@ -228,29 +267,6 @@
         fetch = pltpu.make_async_copy(source, target, isem.at[at])
         fetch.start()
         fetched.append(fetch)
-    barrier = pltpu.get_barrier_semaphore()
-
-    others = []
-    for k in sorted(range(ns), key=lambda k: -min(k, ns - k)):
-        for g in range(ng):
-            if k or g:
-                others.append((lax.rem(si + k, ns), lax.rem(gi + g, ng)))
-    for other in others:
-        pl.semaphore_signal(barrier, inc=1, device_id=other, device_id_type=MESH)
-
-    sub, lane = sub_index(), lane_index()
-    upper = sub < 4
-
-    steps = [(-1, 0), (1, 0), (0, -1), (0, 1), (-1, -1), (-1, 1), (1, -1), (1, 1)]
-
-    def inside(ds, dg):
-        ok = None
-        if ds:
-            ok = (si >= 1) if ds < 0 else (si <= ns - 2)
-        if dg:
-            more = (gi >= 1) if dg < 0 else (gi <= ng - 2)
-            ok = more if ok is None else jnp.logical_and(ok, more)
-        return ok
 
     def copies(ea, dst_a, stage, land, send, recv, low=0, high=None, ways=8, reach=REACH, depth=None):
         depth = reach if depth is None else depth
@@ -459,15 +475,21 @@
     third = copies(rqa, rqa, s3, h3, send3, recv3, 0, 3, 4, 1, REACH)
     outer = copies(rqa, rqa, s3, h3, sendq, recvq, 3, 6, 2, REACH - 1, REACH)
     wedges = wedge_copies()
-    pl.semaphore_wait(barrier, count - 1)
+    meet(barrier, 1)
     begin(zeroth)
     begin(corners)
     begin(first)
     begin(rest)
+    greet(known.at[0], rounds[0])
     turn_out(rows[3], outb.at[3])
     inb[3, si] = outb[3, si]
+    for at in range(len(rounds) - 2):
+        meet(known.at[at], rounds[at])
+        greet(known.at[at + 1], rounds[at + 1])
     finish_recv(zeroth, recv0)
     corner_unpack(corners)
+    meet(known.at[len(rounds) - 2], rounds[-2])
+    greet(known.at[len(rounds) - 1], rounds[-1])
 
     def open0(i, _):
         e1b[6, 2 * i], e1b[6, 2 * i + 1] = unpack(h1, 6, i)
@@ -527,7 +549,6 @@
     finish_recv(first, recv1)
     finish_recv(rest, recv4)
     begin(second)
-    spread_out(outb.at[3], inb.at[3], 3)
     lax.fori_loop(0, (X + 2 * HALO) // 2, open1, 0)
 
     def operate(x, va, vb, base, both=True):
@@ -605,6 +626,8 @@
             row = jnp.where(one == at, value, row)
         gath[step, me] = row
 
+        if step == 0:
+            meet(known.at[len(rounds) - 1], rounds[-1])
         for other in others:
             pltpu.make_async_remote_copy(
                 src_ref=gath.at[step, me], dst_ref=gath.at[step, me], send_sem=asend.at[step], recv_sem=arecv.at[step],
@@ -626,7 +649,7 @@
         curved = down(rest * rest * rq - alpha * rest * mix + alpha * alpha * wt)
         ratio = after / norm
         beta = after / (curved - ratio * after / alpha)
-        return alpha + beta * (1.0 + ratio), -beta * alpha
+        return jnp.broadcast_to(alpha + beta * (1.0 + ratio), (8, 128)), jnp.broadcast_to(-beta * alpha, (8, 128))
 
     def drain(step):
         block = gath.at[step, pl.ds(0, count - 1)]
@@ -659,6 +682,7 @@
         begin(outer)
 
     solve(0, e1a, e1b, lambda c, x: (e1a[3 + c, x], e1b[3 + c, x]), ship_halo)
+    spread_out(outb.at[3], inb.at[3], 3)
     finish_recv(second, recv2)
 
     def open2(i, _):
@@ -698,12 +722,8 @@
             u1a[c, x] = e1a[c, x] + (c0 * rqa[c, x] + c1 * rqa[3 + c, x])
             u1b[c, x] = e1b[c, x] + (c0 * rqb[c, x] + c1 * rqb[3 + c, x]) if both else jnp.zeros((8, 128), jnp.float32)
 
-    def step1_pair(i, _):
-        step1(2 * i)
-        step1(2 * i + 1)
-        return 0
-
-    lax.fori_loop(HALO // 2 - 1, (HALO + X) // 2 + 1, step1_pair, 0)
+    for x in range(HALO - REACH + 1, HALO + X + REACH - 1):
+        step1(x)
     step1(HALO - REACH, False)
     step1(HALO + X + REACH - 1, False)
     finish_send(zeroth)
@@ -868,7 +888,7 @@
             ext(3), ext(3), stage(3), land(3),
             ext(6), ext(6), stage(3), land(3), vm(2, 2, 3, 1, Y, Z),
             ext(3), ext(3), vm(Y, zrows, X * ns), ext(3), ext(3), ext(5), ext(5),
-            vm(2, ns * ng, 1, 128), vm(5, Y * X, Z), vm(4, ns, zrows, 128), vm(4, ns, zrows, 128), vm(ns, 8, 128), vm(ns, 8, 128), vm(6, Y * zrows, X * ns),
+            pltpu.SemaphoreType.REGULAR((4,)), vm(2, ns * ng, 1, 128), vm(5, Y * X, Z), vm(4, ns, zrows, 128), vm(4, ns, zrows, 128), vm(ns, 8, 128), vm(ns, 8, 128), vm(6, Y * zrows, X * ns),
             vm(2, 2, 4, Y, Z), vm(2, 2, 4, Y, Z), dma((4,)), dma((4,)), dma((4,)), dma((4,)),
             dma((4,)), dma((4,)), dma((4,)), dma((4,)), dma((8,)), dma((8,)), dma((4,)), dma((4,)), dma((2,)), dma((2,)), dma((4,)), dma((4,)),
             dma((2,)), dma((2,)), dma((5,)), dma((5,)),

time: 36.1 us -> 33.3 us (0.922)
  Pallas kernels: 35.3 us -> 32.4 us
    pallas_call x1, Pallas kernels: 34.5 us -> 31.6 us  [fused(): pl.pallas_call(lambda *refs: kernel(ns, ng, *refs), name='lattice', out_s...]
where the time goes in v5:
time: 33.3 us; the launch traced here: 33.1 us
  Pallas kernels  32.4 us (97%)
  between operations  0.64 us (2%)
    pallas_call x1, Pallas kernels, fused(): pl.pallas_call(lambda *refs: kernel(ns, ng, *refs), name='lattice', out_s...  31.6 us
    pallas_call x1, Pallas kernels, fused(): pl.pallas_call(store, name='store', out_shape=tuple((jax.ShapeDtypeStruct...  0.83 us

profile of v5, /device:TPU:0, one launch (start us, length us, event | category | flops | bytes accessed | tf_op | source)
XLA Modules:
  0.0 33.1 jit_solution(10006477045985569408)
XLA Ops:
  0.6 31.6 %lattice.1 = (f32[3,16,8,128]{3,2,1,0:T(8,128)S(1)}, f32[6,128,128]{2,1,0:T(8,128)S(1)}) custom-call(f32[3,16,8,128]{3,2,1,0:T(8,128)} %refs_0_.1, f32[3,16,8,128]{3,2,1,0:T(8,128)} %refs_1_.1, f32[3,16,8,128]{3,2,1,0:T(8,128)} %refs_2_.1, f32[16,8,128]{2,1,0:T(8,128)} %refs_3_.1, s32[4,2,32]{2,1,0:T(2,128)} %refs_4_.1, s32[4,2,32]{2,1,0:T(2,128)} %refs_5_.1, ...), custom_call_target="tpu_custom_call" | custom-call | tf_op jit(solution)/shard_map/lattice/pallas_call | solution.py:877
  32.2 0.8 %store.1 = (f32[3,16,8,128]{3,2,1,0:T(8,128)}, f32[6,128,128]{2,1,0:T(8,128)}) custom-call(f32[3,16,8,128]{3,2,1,0:T(8,128)S(1)} %get-tuple-element.6.disp_in, f32[6,128,128]{2,1,0:T(8,128)S(1)} %get-tuple-element.7.coef_in), custom_call_target="tpu_custom_call" | custom-call | tf_op jit(solution)/shard_map/store/pallas_call | solution.py:898

commit v6 on v5

--- a/solution.py
+++ b/solution.py
@@ -222,11 +222,20 @@
     count = ns * ng
     barrier = pltpu.get_barrier_semaphore()
 
+    def mirrored(place, mask, length):
+        bit, result = 1, 0
+        while bit < length:
+            here = place // bit % 2
+            result = result + bit * (1 - here if mask // bit % 2 else here)
+            bit *= 2
+        return result
+
     others = []
     for k in sorted(range(ns), key=lambda k: -min(k, ns - k)):
         for g in range(ng):
             if k or g:
                 others.append((lax.rem(si + k, ns), lax.rem(gi + g, ng)))
+
     sub, lane = sub_index(), lane_index()
     upper = sub < 4
 
@@ -394,11 +403,10 @@
         turned = value.T
         for j in range(ns):
             out[j] = turned[j * zrows:(j + 1) * zrows]
-        return turned
 
     def spread_out(source, target, at):
-        for i in range(1, ns):
-            to = lax.rem(si + i, ns)
+        for m in reversed(range(1, ns)):
+            to = mirrored(si, m, ns)
             pltpu.make_async_remote_copy(
                 src_ref=source.at[to], dst_ref=target.at[si], send_sem=tsend.at[at], recv_sem=trecv.at[at],
                 device_id=(to, gi), device_id_type=MESH).start()
@@ -443,16 +451,29 @@
                 device_id=(si + ds, gi + dg), device_id_type=MESH)))
         return made
 
-    near = sub % 4 < 2
+    def corner_rows(side, end):
+        dx1, dx2 = (0, 4) if end == 0 else (4, 0)
+        dy1, dy2 = (0, 1) if side == 0 else (3, 2)
+        return dx1 + dy1, dx1 + dy2, dx2 + dy1
+
+    def any_row(places):
+        found = sub == places[0]
+        for place in places[1:]:
+            found = jnp.logical_or(found, sub == place)
+        return found
+
+    corner_sets = ((0, 1, (3, 4)), (2, 6, (5,)))
     for side in range(2):
         for end in range(2):
-            for t in range((7 + 1) // 2):
-                tile = s1[side, 2 * t, end * (X // 2 - 1)]
-                if 2 * t + 1 < 7:
-                    other = s1[side, 2 * t + 1, end * (X // 2 - 1)]
-                    tile = (jnp.where(near, tile, pltpu.roll(other, 2, 0)) if side == 0
-                            else jnp.where(near, pltpu.roll(other, 6, 0), tile))
-                ctake[side, end, t] = tile
+            places = corner_rows(side, end)
+            first_here, second_here = any_row(places), any_row([(v + 2) % 8 for v in places])
+            for at, (ch_a, ch_b, right) in enumerate(corner_sets):
+                tiles = [s1[side, ch, end * (X // 2 - 1)] for ch in (ch_a, ch_b) + right]
+                tile = pltpu.roll(tiles[2], 5, 0)
+                if len(right) == 2:
+                    tile = jnp.where(sub == (places[0] + 5) % 8, tile, pltpu.roll(tiles[3], 3 if side else 7, 0))
+                tile = jnp.where(first_here, tiles[0], jnp.where(second_here, pltpu.roll(tiles[1], 2, 0), tile))
+                ctake[side, end, at] = tile
 
     def corner_unpack(made):
         for at, (ds, dg) in enumerate(steps[4:]):
@@ -463,9 +484,13 @@
             @pl.when(inside(ds, dg))
             def _():
                 back.wait_recv()
-                for ch in range(7):
-                    tile = cland[side, end, ch // 2]
-                    h1[side, ch, pair] = tile if ch % 2 == 0 else pltpu.roll(tile, 6 if side == 0 else 2, 0)
+                for at, (ch_a, ch_b, right) in enumerate(corner_sets):
+                    tile = cland[side, end, at]
+                    h1[side, ch_a, pair] = tile
+                    h1[side, ch_b, pair] = pltpu.roll(tile, 6, 0)
+                    h1[side, right[0], pair] = pltpu.roll(tile, 3, 0)
+                    if len(right) == 2:
+                        h1[side, right[1], pair] = pltpu.roll(tile, 5 if side else 1, 0)
 
     corners = corner_copies()
     zeroth = copies(e1a, e1a, s1, h1, send0, recv0, 6, 7, 4)
@@ -739,7 +764,17 @@
         return (MASS_TERM * (2.0 * u1a[c, x] - e1a[c, x]) + e2a[c, x],
                 MASS_TERM * (2.0 * u1b[c, x] - e1b[c, x]) + e2b[c, x])
 
+    def early(at, ref, ch):
+        for x in range(X):
+            rows[at, pl.ds(x, 8, stride=X), :] = ref[ch, HALO + x]
+        turn_out(rows[at], outb.at[at])
+        spread_out(outb.at[at], inb.at[at], at)
+        inb[at, si] = outb[at, si]
+
+    early(2, u1a, 2)
     solve(1, u1a, u1b, rhs2)
+    early(4, rqa, 2)
+    early(5, rqa, 5)
     landed(inb.at[3], trecv.at[3])
     for y, piece in enumerate(regroup([inb[3, j] for j in range(ns)])):
         scale[y] = piece
@@ -760,12 +795,16 @@
         turned = turn_out(rows[c], outb.at[c])
         spread_out(outb.at[c], inb.at[c], c)
         inb[c, si] = outb[c, si]
-        return turned
-
-    def finish_edges(turned):
+
+    def joint(ref, j, low, high):
+        return jnp.concatenate([
+            ref[2, j, at:at + 8] + (c0 * ref[4, j, at:at + 8] + c1 * ref[5, j, at:at + 8])
+            for at in range(low, high, 8)], axis=0)
+
+    def finish_edges():
         for x in range(X):
-            rows[4, pl.ds(x, 8, stride=X), :] = step2(u1b, rqb, 1, HALO + x)
-        sides_y = rows[4].T
+            rows[6, pl.ds(x, 8, stride=X), :] = step2(u1b, rqb, 1, HALO + x)
+        sides_y = rows[6].T
         zero = jnp.zeros((8, 128), jnp.float32)
         for j in range(ns):
             low, high = sides_y[zrows * j:zrows * j + 8], sides_y[zrows * j + 8:zrows * j + 16]
@@ -773,15 +812,17 @@
                              jnp.where(lane < 64, pltpu.roll(pltpu.roll(low, 4, 0), 48, 1),
                                        jnp.where(lane < 96, pltpu.roll(high, 80, 1),
                                                  pltpu.roll(pltpu.roll(high, 4, 0), 112, 1))))
-            before = pltpu.roll(turned[zrows * j - 8:zrows * j], 5, 0) if j else zero
-            after = pltpu.roll(turned[zrows * (j + 1):zrows * (j + 1) + 8], 5, 0) if j + 1 < ns else zero
+            before = pltpu.roll(joint(outb, j - 1, zrows - 8, zrows), 5, 0) if j else zero
+            after = pltpu.roll(joint(outb, j + 1, 0, 8), 5, 0) if j + 1 < ns else zero
             outx[j] = jnp.where(sub == 4, before, jnp.where(sub == 5, after, tile))
-        spread_out(outx, inx, 4)
+        spread_out(outx, inx, 6)
         inx[si] = outx[si]
 
-    finish_edges(finish(2))
     finish(0)
+    finish_edges()
     finish(1)
+    for x in range(X):
+        disp_ref[2, x] = step2(u1a, rqa, 2, HALO + x)
     fetched[7].wait()
 
     c1t, c3t = float(np.sqrt(0.5) * np.cos(np.pi / 8)), float(np.sqrt(0.5) * np.cos(3 * np.pi / 8))
@@ -808,24 +849,26 @@
         landed(inb.at[c], trecv.at[c])
         return regroup([inb[c, j] for j in range(ns)])
 
-    field = arrived(2)
-    encode(2, field)
-    landed(inx, trecv.at[4])
+    for at in (2, 4, 5):
+        landed(inb.at[at], trecv.at[at])
+    along = regroup([joint(inb, j, 0, zrows) for j in range(ns)])
+    encode(2, along)
+    field = arrived(0)
+    encode(0, field)
+    wide = lax.broadcasted_iota(jnp.int32, (zrows, 128), 1)
+    encode(3, [scale[y] * (jnp.where(wide < 127, up_z(field[y]), 0.0) - jnp.where(wide > 0, down_z(field[y]), 0.0))
+               for y in range(Y)])
+    landed(inx, trecv.at[6])
     edges = regroup([inx[j] for j in range(ns)])
     stress = []
     for y in range(Y):
-        low, high = field[y][0:8], field[y][8:16]
+        low, high = along[y][0:8], along[y][8:16]
         ul, uh, dl, dh = pltpu.roll(low, 7, 0), pltpu.roll(high, 7, 0), pltpu.roll(low, 1, 0), pltpu.roll(high, 1, 0)
         first, last = sub == 0, sub == 7
         low = jnp.where(last, uh, ul) - jnp.where(first, pltpu.roll(edges[y], 4, 0), dl)
         high = jnp.where(last, pltpu.roll(edges[y], 2, 0), uh) - jnp.where(first, dl, dh)
         stress.append(scale[y] * jnp.concatenate([low, high], axis=0))
     encode(5, stress)
-    field = arrived(0)
-    encode(0, field)
-    wide = lax.broadcasted_iota(jnp.int32, (zrows, 128), 1)
-    encode(3, [scale[y] * (jnp.where(wide < 127, up_z(field[y]), 0.0) - jnp.where(wide > 0, down_z(field[y]), 0.0))
-               for y in range(Y)])
     field = arrived(1)
     encode(1, field)
     outside = []
@@ -836,9 +879,9 @@
     encode(4, [scale[y] * (field[y + 2] - field[y]) for y in range(Y)])
     drain(0)
     drain(1)
-    for at in range(4):
+    for at in range(6):
         landed(inb.at[at], tsend.at[at])
-    landed(inx, tsend.at[4])
+    landed(inx, tsend.at[6])
 
 
 def store(disp_in, coef_in, disp_out, coef_out, sems):
@@ -888,10 +931,10 @@
             ext(3), ext(3), stage(3), land(3),
             ext(6), ext(6), stage(3), land(3), vm(2, 2, 3, 1, Y, Z),
             ext(3), ext(3), vm(Y, zrows, X * ns), ext(3), ext(3), ext(5), ext(5),
-            pltpu.SemaphoreType.REGULAR((4,)), vm(2, ns * ng, 1, 128), vm(5, Y * X, Z), vm(4, ns, zrows, 128), vm(4, ns, zrows, 128), vm(ns, 8, 128), vm(ns, 8, 128), vm(6, Y * zrows, X * ns),
-            vm(2, 2, 4, Y, Z), vm(2, 2, 4, Y, Z), dma((4,)), dma((4,)), dma((4,)), dma((4,)),
+            pltpu.SemaphoreType.REGULAR((4,)), vm(2, ns * ng, 1, 128), vm(7, Y * X, Z), vm(6, ns, zrows, 128), vm(6, ns, zrows, 128), vm(ns, 8, 128), vm(ns, 8, 128), vm(6, Y * zrows, X * ns),
+            vm(2, 2, 2, Y, Z), vm(2, 2, 2, Y, Z), dma((4,)), dma((4,)), dma((4,)), dma((4,)),
             dma((4,)), dma((4,)), dma((4,)), dma((4,)), dma((8,)), dma((8,)), dma((4,)), dma((4,)), dma((2,)), dma((2,)), dma((4,)), dma((4,)),
-            dma((2,)), dma((2,)), dma((5,)), dma((5,)),
+            dma((2,)), dma((2,)), dma((7,)), dma((7,)),
         ],
         compiler_params=pltpu.CompilerParams(collective_id=0, has_side_effects=True, vmem_limit_bytes=24 << 20),
     )(*operands)

time: 33.3 us -> 31.9 us (0.958)
  Pallas kernels: 32.4 us -> 31 us
    pallas_call x1, Pallas kernels: 31.6 us -> 30.2 us  [fused(): pl.pallas_call(lambda *refs: kernel(ns, ng, *refs), name='lattice', out_s...]
where the time goes in v6:
time: 31.9 us; the launch traced here: 31.7 us
  Pallas kernels  31 us (97%)
  between operations  0.64 us (2%)
    pallas_call x1, Pallas kernels, fused(): pl.pallas_call(lambda *refs: kernel(ns, ng, *refs), name='lattice', out_s...  30.2 us
    pallas_call x1, Pallas kernels, fused(): pl.pallas_call(store, name='store', out_shape=tuple((jax.ShapeDtypeStruct...  0.83 us

profile of v6, /device:TPU:0, one launch (start us, length us, event | category | flops | bytes accessed | tf_op | source)
XLA Modules:
  0.0 31.7 jit_solution(11257726992544893990)
XLA Ops:
  0.6 30.2 %lattice.1 = (f32[3,16,8,128]{3,2,1,0:T(8,128)S(1)}, f32[6,128,128]{2,1,0:T(8,128)S(1)}) custom-call(f32[3,16,8,128]{3,2,1,0:T(8,128)} %refs_0_.1, f32[3,16,8,128]{3,2,1,0:T(8,128)} %refs_1_.1, f32[3,16,8,128]{3,2,1,0:T(8,128)} %refs_2_.1, f32[16,8,128]{2,1,0:T(8,128)} %refs_3_.1, s32[4,2,32]{2,1,0:T(2,128)} %refs_4_.1, s32[4,2,32]{2,1,0:T(2,128)} %refs_5_.1, ...), custom_call_target="tpu_custom_call" | custom-call | tf_op jit(solution)/shard_map/lattice/pallas_call | solution.py:920
  30.8 0.8 %store.1 = (f32[3,16,8,128]{3,2,1,0:T(8,128)}, f32[6,128,128]{2,1,0:T(8,128)}) custom-call(f32[3,16,8,128]{3,2,1,0:T(8,128)S(1)} %get-tuple-element.6.disp_in, f32[6,128,128]{2,1,0:T(8,128)S(1)} %get-tuple-element.7.coef_in), custom_call_target="tpu_custom_call" | custom-call | tf_op jit(solution)/shard_map/store/pallas_call | solution.py:941

commit v7 on v6

--- a/solution.py
+++ b/solution.py
@@ -213,9 +213,9 @@
 def kernel(ns, ng, u_in, p_in, f_in, k_in, br_in, fl_in, ez_in, gt_in,
            disp_ref, coef_ref,
            u_ref, p_ref, f_ref, k_ref, br_ref, fl_ref, ez_ref, gt_ref, isem,
-           e1a, e1b, s1, h1, e2a, e2b, s2, h2, rqa, rqb, s3, h3, k3,
+           e1a, e1b, s1, h1, e2a, e2b, s2, h2, rqa, rqb, s3, h3, k3, ends,
            u1a, u1b, scale, dga, dgb, kca, kcb, known, gath, rows, outb, inb, outx, inx, work,
-           ctake, cland, csend, crecv, send4, recv4, send0, recv0, send1, recv1, send2, recv2, send3, recv3, sendq, recvq, sendk, recvk, asend, arecv, tsend, trecv):
+           ctake, cland, csend, crecv, send4, recv4, send0, recv0, send1, recv1, send2, recv2, send3, recv3, sendq, recvq, sendk, recvk, sendu, recvu, sendw, recvw, ftake, fland, sendf, recvf, asend, arecv, tsend, trecv):
     X, Y, Z = u_ref.shape[1:]
     si, gi = lax.axis_index("slab"), lax.axis_index("grp")
     me = si * ng + gi
@@ -277,7 +277,7 @@
         fetch.start()
         fetched.append(fetch)
 
-    def copies(ea, dst_a, stage, land, send, recv, low=0, high=None, ways=8, reach=REACH, depth=None):
+    def copies(ea, dst_a, stage, land, send, recv, low=0, high=None, ways=8, reach=REACH, depth=None, ends=None):
         depth = reach if depth is None else depth
         half = X // 2
         edge = HALO // 2
@@ -285,7 +285,10 @@
         chans = pl.ds(low, (ea.shape[0] if high is None else high) - low)
         for at, (ds, dg) in enumerate(steps[:ways]):
             if dg == 0:
-                if ds < 0:
+                if ends is not None:
+                    source = ends.at[0 if ds < 0 else 1]
+                    target = dst_a.at[chans, pl.ds(HALO + X if ds < 0 else HALO - depth, reach)]
+                elif ds < 0:
                     source = ea.at[chans, pl.ds(HALO + depth - reach, reach)]
                     target = dst_a.at[chans, pl.ds(HALO + X + depth - reach, reach)]
                 else:
@@ -430,6 +433,58 @@
             gap //= 2
         return pieces
 
+    not_last, not_first = lane < 127, lane > 0
+
+    def inner_ends():
+        for end, x in ((0, HALO + 1), (1, HALO + X - 2)):
+            w = e1a[6, x]
+            along = (0.5 * (w + e1a[6, x + 1]), 0.5 * (w + e1a[6, x - 1]),
+                     jnp.where(sub < 7, 0.5 * (w + pltpu.roll(w, 7, 0)), 0.0),
+                     jnp.where(sub > 0, 0.5 * (w + pltpu.roll(w, 1, 0)), 0.0),
+                     0.5 * (w + jnp.where(not_last, up_z(w), 0.0)), 0.5 * (w + jnp.where(not_first, down_z(w), 0.0)))
+            for c in range(3):
+                v = e1a[c, x]
+                parts = (along[0] * (v - e1a[c, x + 1]) + along[1] * (v - e1a[c, x - 1]),
+                         along[2] * (v - pltpu.roll(v, 7, 0)) + along[3] * (v - pltpu.roll(v, 1, 0)),
+                         along[4] * (v - jnp.where(not_last, up_z(v), 0.0))
+                         + along[5] * (v - jnp.where(not_first, down_z(v), 0.0)))
+                image = MASS_TERM * v + (SPRING_SHEAR * (parts[0] + parts[1] + parts[2]) + SHEAR_REST * parts[c])
+                ends[end, c, 1 - end] = e1a[3 + c, x] - image
+                ends[end, c, end] = e1a[3 + c, x - 1 + 2 * end]
+
+    def outer_residual(x):
+        wa, wb = e1a[6, x], e1b[6, x]
+        above = jnp.where(sub == 7, 0.5 * (wa + up_y(wa, wb)[0]), 0.0)
+        below = jnp.where(sub == 0, 0.5 * (wa + down_y(wa, wb)[0]), 0.0)
+        for c in range(3):
+            a, b = e1a[c, x], e1b[c, x]
+            change = above * (a - up_y(a, b)[0]) + below * (a - down_y(a, b)[0])
+            rqa[c, x] = e1a[3 + c, x] - (SPRING_NORMAL if c == 1 else SPRING_SHEAR) * change
+            rqb[c, x] = jnp.zeros((8, 128), jnp.float32)
+
+    def tip_copies():
+        made = []
+        for at, (ds, dg) in enumerate(steps[4:]):
+            side, end = (0 if dg < 0 else 1), (0 if ds < 0 else 1)
+            made.append((ds, dg, pltpu.make_async_remote_copy(
+                src_ref=ftake.at[side, end], dst_ref=fland.at[side, 1 - end],
+                send_sem=sendf.at[at], recv_sem=recvf.at[3 - at],
+                device_id=(si + ds, gi + dg), device_id_type=MESH)))
+        return made
+
+    def tip_unpack(made):
+        for at, (ds, dg) in enumerate(steps[4:]):
+            side, end = (0 if dg > 0 else 1), (1 if ds > 0 else 0)
+            pair = HALO // 2 + X // 2 if ds > 0 else HALO // 2 - 1
+            back = made[3 - at][2]
+
+            @pl.when(inside(ds, dg))
+            def _():
+                back.wait_recv()
+                tile = fland[side, end]
+                for c in range(3):
+                    h2[side, c, pair] = pltpu.roll(tile, 8 - 2 * c, 0) if c else tile
+
     def wedge_copies():
         made = []
         for at, (ds, dg) in enumerate(steps[4:]):
@@ -474,6 +529,9 @@
                     tile = jnp.where(sub == (places[0] + 5) % 8, tile, pltpu.roll(tiles[3], 3 if side else 7, 0))
                 tile = jnp.where(first_here, tiles[0], jnp.where(second_here, pltpu.roll(tiles[1], 2, 0), tile))
                 ctake[side, end, at] = tile
+            near = [s2[side, c, end * (X // 2 - 1)] for c in range(3)]
+            ftake[side, end] = jnp.where(sub == places[0], near[0], jnp.where(
+                sub == (places[0] + 2) % 8, pltpu.roll(near[1], 2, 0), pltpu.roll(near[2], 4, 0)))
 
     def corner_unpack(made):
         for at, (ds, dg) in enumerate(steps[4:]):
@@ -493,10 +551,13 @@
                         h1[side, right[1], pair] = pltpu.roll(tile, 5 if side else 1, 0)
 
     corners = corner_copies()
-    zeroth = copies(e1a, e1a, s1, h1, send0, recv0, 6, 7, 4)
-    first = copies(e1a, e1a, s1, h1, send1, recv1, 0, 3, 4)
-    rest = copies(e1a, e1a, s1, h1, send4, recv4, 3, 6, 4, REACH - 1)
-    second = copies(e2a, e2a, s2, h2, send2, recv2, reach=REACH - 1)
+    zeroth = copies(e1a, e1a, s1, h1, send0, recv0, 6, 7, 4, REACH - 1)
+    first = copies(e1a, e1a, s1, h1, send1, recv1, 0, 3, 4, REACH - 1)
+    rest = copies(e1a, e1a, s1, h1, send4, recv4, 3, 6, 4, REACH - 1, None, ends)
+    late = (copies(e1a, e1a, s1, h1, sendu, recvu, 0, 3, 2, 1, REACH),
+            copies(e1a, e1a, s1, h1, sendw, recvw, 6, 7, 2, 1, REACH))
+    second = copies(e2a, e2a, s2, h2, send2, recv2, 0, 3, 4, REACH - 1)
+    tips = tip_copies()
     third = copies(rqa, rqa, s3, h3, send3, recv3, 0, 3, 4, 1, REACH)
     outer = copies(rqa, rqa, s3, h3, sendq, recvq, 3, 6, 2, REACH - 1, REACH)
     wedges = wedge_copies()
@@ -504,6 +565,7 @@
     begin(zeroth)
     begin(corners)
     begin(first)
+    inner_ends()
     begin(rest)
     greet(known.at[0], rounds[0])
     turn_out(rows[3], outb.at[3])
@@ -530,7 +592,6 @@
     def link(w, other):
         return jnp.where(jnp.minimum(w, other) > 0.0, (0.5 * SPRING_SHEAR) * (w + other), 0.0)
 
-    not_last, not_first = lane < 127, lane > 0
 
     def over_rows(low, high, width, body, carried=0):
         width = max(v for v in range(1, width + 1) if (high - low) % v == 0)
@@ -568,12 +629,18 @@
             dg[1, x] = every + SHEAR_REST * sy
             dg[2, x] = every + SHEAR_REST * sz
 
-    kca[0, HALO - REACH] = link(e1a[6, HALO - REACH], e1a[6, HALO - REACH + 1])
-    kcb[0, HALO - REACH] = link(e1b[6, HALO - REACH], e1b[6, HALO - REACH + 1])
-    over_rows(HALO - 2, HALO + X + 2, WIDE_K, all_coefficients)
+    def edge_link(x):
+        kca[0, x] = link(e1a[6, x], e1a[6, x + 1])
+        kcb[0, x] = link(e1b[6, x], e1b[6, x + 1])
+
+    edge_link(HALO - 2)
+    over_rows(HALO - 1, HALO + X + 1, WIDE_K, all_coefficients)
     finish_recv(first, recv1)
     finish_recv(rest, recv4)
     begin(second)
+    begin(tips)
+    for made in late:
+        begin(made)
     lax.fori_loop(0, (X + 2 * HALO) // 2, open1, 0)
 
     def operate(x, va, vb, base, both=True):
@@ -596,7 +663,7 @@
             result.append(pair)
         return result
 
-    def solve(step, va, vb, rhs_of, ship_halo=None):
+    def solve(step, va, vb, rhs_of, reach, ship_halo=None):
         def residual(rows_here, _):
             for x in rows_here:
                 image = operate(x, va, vb, 0)
@@ -606,7 +673,7 @@
                     rqb[c, x] = rb - image[c][1]
             return 0
 
-        over_rows(HALO - 2, HALO + X + 2, WIDE_R, residual)
+        over_rows(HALO - reach, HALO + X + reach, WIDE_R, residual)
 
         def put(x, image):
             for c in range(3):
@@ -706,9 +773,17 @@
         begin(wedges)
         begin(outer)
 
-    solve(0, e1a, e1b, lambda c, x: (e1a[3 + c, x], e1b[3 + c, x]), ship_halo)
+    outer_residual(HALO - 2)
+    outer_residual(HALO + X + 1)
+    solve(0, e1a, e1b, lambda c, x: (e1a[3 + c, x], e1b[3 + c, x]), 1, ship_halo)
     spread_out(outb.at[3], inb.at[3], 3)
     finish_recv(second, recv2)
+    tip_unpack(tips)
+    for made, recv in zip(late, (recvu, recvw)):
+        finish_recv(made, recv)
+    edge_link(HALO - REACH)
+    coefficients(HALO - 2)
+    coefficients(HALO + X + 1)
 
     def open2(i, _):
         for ch in range(3):
@@ -756,6 +831,9 @@
     finish_send(rest)
     finish_send(first)
     finish_send(second)
+    finish_send(tips)
+    for made in late:
+        finish_send(made)
     finish_send(third)
     finish_send(outer)
     finish_send(wedges)
@@ -772,12 +850,9 @@
         inb[at, si] = outb[at, si]
 
     early(2, u1a, 2)
-    solve(1, u1a, u1b, rhs2)
+    solve(1, u1a, u1b, rhs2, 2)
     early(4, rqa, 2)
     early(5, rqa, 5)
-    landed(inb.at[3], trecv.at[3])
-    for y, piece in enumerate(regroup([inb[3, j] for j in range(ns)])):
-        scale[y] = piece
     c0, c1 = collect(1)
 
     def step2(ra, rb, c, x):
@@ -853,6 +928,9 @@
         landed(inb.at[at], trecv.at[at])
     along = regroup([joint(inb, j, 0, zrows) for j in range(ns)])
     encode(2, along)
+    landed(inb.at[3], trecv.at[3])
+    for y, piece in enumerate(regroup([inb[3, j] for j in range(ns)])):
+        scale[y] = piece
     field = arrived(0)
     encode(0, field)
     wide = lax.broadcasted_iota(jnp.int32, (zrows, 128), 1)
@@ -929,11 +1007,12 @@
             vm(*ez.shape), pltpu.VMEM(gt.shape, gt.dtype), pltpu.SemaphoreType.DMA((8,)),
             ext(7), ext(7), stage(7), land(7),
             ext(3), ext(3), stage(3), land(3),
-            ext(6), ext(6), stage(3), land(3), vm(2, 2, 3, 1, Y, Z),
+            ext(6), ext(6), stage(3), land(3), vm(2, 2, 3, 1, Y, Z), vm(2, 3, 2, Y, Z),
             ext(3), ext(3), vm(Y, zrows, X * ns), ext(3), ext(3), ext(5), ext(5),
             pltpu.SemaphoreType.REGULAR((4,)), vm(2, ns * ng, 1, 128), vm(7, Y * X, Z), vm(6, ns, zrows, 128), vm(6, ns, zrows, 128), vm(ns, 8, 128), vm(ns, 8, 128), vm(6, Y * zrows, X * ns),
             vm(2, 2, 2, Y, Z), vm(2, 2, 2, Y, Z), dma((4,)), dma((4,)), dma((4,)), dma((4,)),
-            dma((4,)), dma((4,)), dma((4,)), dma((4,)), dma((8,)), dma((8,)), dma((4,)), dma((4,)), dma((2,)), dma((2,)), dma((4,)), dma((4,)),
+            dma((4,)), dma((4,)), dma((4,)), dma((4,)), dma((4,)), dma((4,)), dma((4,)), dma((4,)), dma((2,)), dma((2,)), dma((4,)), dma((4,)),
+            dma((2,)), dma((2,)), dma((2,)), dma((2,)), vm(2, 2, Y, Z), vm(2, 2, Y, Z), dma((4,)), dma((4,)),
             dma((2,)), dma((2,)), dma((7,)), dma((7,)),
         ],
         compiler_params=pltpu.CompilerParams(collective_id=0, has_side_effects=True, vmem_limit_bytes=24 << 20),

time: 31.9 us -> 31.3 us (0.981)
  Pallas kernels: 31 us -> 30.4 us
    pallas_call x1, Pallas kernels: 30.2 us -> 29.6 us  [fused(): pl.pallas_call(lambda *refs: kernel(ns, ng, *refs), name='lattice', out_s...]
where the time goes in v7:
time: 31.3 us; the launch traced here: 31.1 us
  Pallas kernels  30.4 us (97%)
  between operations  0.64 us (2%)
    pallas_call x1, Pallas kernels, fused(): pl.pallas_call(lambda *refs: kernel(ns, ng, *refs), name='lattice', out_s...  29.6 us
    pallas_call x1, Pallas kernels, fused(): pl.pallas_call(store, name='store', out_shape=tuple((jax.ShapeDtypeStruct...  0.83 us

profile of v7, /device:TPU:0, one launch (start us, length us, event | category | flops | bytes accessed | tf_op | source)
XLA Modules:
  0.0 31.1 jit_solution(14244883380638512636)
XLA Ops:
  0.6 29.6 %lattice.1 = (f32[3,16,8,128]{3,2,1,0:T(8,128)S(1)}, f32[6,128,128]{2,1,0:T(8,128)S(1)}) custom-call(f32[3,16,8,128]{3,2,1,0:T(8,128)} %refs_0_.1, f32[3,16,8,128]{3,2,1,0:T(8,128)} %refs_1_.1, f32[3,16,8,128]{3,2,1,0:T(8,128)} %refs_2_.1, f32[16,8,128]{2,1,0:T(8,128)} %refs_3_.1, s32[4,2,32]{2,1,0:T(2,128)} %refs_4_.1, s32[4,2,32]{2,1,0:T(2,128)} %refs_5_.1, ...), custom_call_target="tpu_custom_call" | custom-call | tf_op jit(solution)/shard_map/lattice/pallas_call | solution.py:998
  30.3 0.8 %store.1 = (f32[3,16,8,128]{3,2,1,0:T(8,128)}, f32[6,128,128]{2,1,0:T(8,128)}) custom-call(f32[3,16,8,128]{3,2,1,0:T(8,128)S(1)} %get-tuple-element.6.disp_in, f32[6,128,128]{2,1,0:T(8,128)S(1)} %get-tuple-element.7.coef_in), custom_call_target="tpu_custom_call" | custom-call | tf_op jit(solution)/shard_map/store/pallas_call | solution.py:1020

commit v8 on v7

--- a/solution.py
+++ b/solution.py
@@ -577,6 +577,10 @@
     corner_unpack(corners)
     meet(known.at[len(rounds) - 2], rounds[-2])
     greet(known.at[len(rounds) - 1], rounds[-1])
+    begin(second)
+    begin(tips)
+    for made in late:
+        begin(made)
 
     def open0(i, _):
         e1b[6, 2 * i], e1b[6, 2 * i + 1] = unpack(h1, 6, i)
@@ -637,10 +641,6 @@
     over_rows(HALO - 1, HALO + X + 1, WIDE_K, all_coefficients)
     finish_recv(first, recv1)
     finish_recv(rest, recv4)
-    begin(second)
-    begin(tips)
-    for made in late:
-        begin(made)
     lax.fori_loop(0, (X + 2 * HALO) // 2, open1, 0)
 
     def operate(x, va, vb, base, both=True):

time: 31.3 us -> 31.2 us (level)
  no operation moved by 1% of the time
where the time goes in v8:
time: 31.2 us; the launch traced here: 31.1 us
  Pallas kernels  30.4 us (97%)
  between operations  0.64 us (2%)
    pallas_call x1, Pallas kernels, fused(): pl.pallas_call(lambda *refs: kernel(ns, ng, *refs), name='lattice', out_s...  29.6 us
    pallas_call x1, Pallas kernels, fused(): pl.pallas_call(store, name='store', out_shape=tuple((jax.ShapeDtypeStruct...  0.83 us

profile of v8, /device:TPU:0, one launch (start us, length us, event | category | flops | bytes accessed | tf_op | source)
XLA Modules:
  0.0 31.1 jit_solution(13657434381232195487)
XLA Ops:
  0.6 29.6 %lattice.1 = (f32[3,16,8,128]{3,2,1,0:T(8,128)S(1)}, f32[6,128,128]{2,1,0:T(8,128)S(1)}) custom-call(f32[3,16,8,128]{3,2,1,0:T(8,128)} %refs_0_.1, f32[3,16,8,128]{3,2,1,0:T(8,128)} %refs_1_.1, f32[3,16,8,128]{3,2,1,0:T(8,128)} %refs_2_.1, f32[16,8,128]{2,1,0:T(8,128)} %refs_3_.1, s32[4,2,32]{2,1,0:T(2,128)} %refs_4_.1, s32[4,2,32]{2,1,0:T(2,128)} %refs_5_.1, ...), custom_call_target="tpu_custom_call" | custom-call | tf_op jit(solution)/shard_map/lattice/pallas_call | solution.py:998
  30.2 0.8 %store.1 = (f32[3,16,8,128]{3,2,1,0:T(8,128)}, f32[6,128,128]{2,1,0:T(8,128)}) custom-call(f32[3,16,8,128]{3,2,1,0:T(8,128)S(1)} %get-tuple-element.6.disp_in, f32[6,128,128]{2,1,0:T(8,128)S(1)} %get-tuple-element.7.coef_in), custom_call_target="tpu_custom_call" | custom-call | tf_op jit(solution)/shard_map/store/pallas_call | solution.py:1020

commit v9 on v8

--- a/solution.py
+++ b/solution.py
@@ -214,8 +214,8 @@
            disp_ref, coef_ref,
            u_ref, p_ref, f_ref, k_ref, br_ref, fl_ref, ez_ref, gt_ref, isem,
            e1a, e1b, s1, h1, e2a, e2b, s2, h2, rqa, rqb, s3, h3, k3, ends,
-           u1a, u1b, scale, dga, dgb, kca, kcb, known, gath, rows, outb, inb, outx, inx, work,
-           ctake, cland, csend, crecv, send4, recv4, send0, recv0, send1, recv1, send2, recv2, send3, recv3, sendq, recvq, sendk, recvk, sendu, recvu, sendw, recvw, ftake, fland, sendf, recvf, asend, arecv, tsend, trecv):
+           u1a, u1b, sa, sb, scale, dga, dgb, kca, kcb, known, gath, rows, outb, inb, outx, inx, work,
+           blanks, sends, ctake, cland, crecv, recv0, recv1, recv2, recv3, recvk, ftake, fland, recvf, asend, arecv, tsend, trecv):
     X, Y, Z = u_ref.shape[1:]
     si, gi = lax.axis_index("slab"), lax.axis_index("grp")
     me = si * ng + gi
@@ -273,11 +273,11 @@
         (br_in, br_ref), (fl_in, fl_ref), (ez_in, ez_ref), (k_in, k_ref), (u_in, u_ref), (p_in, p_ref),
         (f_in, f_ref), (gt_in, gt_ref),
     )):
-        fetch = pltpu.make_async_copy(source, target, isem.at[at])
+        fetch = pltpu.make_async_copy(source, target, isem.at[min(at, 4) if at < 7 else 5])
         fetch.start()
         fetched.append(fetch)
 
-    def copies(ea, dst_a, stage, land, send, recv, low=0, high=None, ways=8, reach=REACH, depth=None, ends=None):
+    def copies(ea, dst_a, stage, land, recv, low=0, high=None, ways=4, reach=REACH, depth=None, ends=None):
         depth = reach if depth is None else depth
         half = X // 2
         edge = HALO // 2
@@ -296,16 +296,9 @@
                     target = dst_a.at[chans, pl.ds(HALO - depth, reach)]
             else:
                 side = 0 if dg < 0 else 1
-                if ds == 0:
-                    source, target = stage.at[side, chans], land.at[side, chans, pl.ds(edge, half)]
-                elif ds < 0:
-                    source = stage.at[side, chans, pl.ds(0, 1)]
-                    target = land.at[side, chans, pl.ds(edge + half, 1)]
-                else:
-                    source = stage.at[side, chans, pl.ds(half - 1, 1)]
-                    target = land.at[side, chans, pl.ds(edge - 1, 1)]
+                source, target = stage.at[side, chans], land.at[side, chans, pl.ds(edge, half)]
             made.append((ds, dg, pltpu.make_async_remote_copy(
-                src_ref=source, dst_ref=target, send_sem=send.at[at], recv_sem=recv.at[at ^ 1 if at < 4 else 11 - at],
+                src_ref=source, dst_ref=target, send_sem=sends.at[at], recv_sem=recv.at[at ^ 1],
                 device_id=(si + ds, gi + dg), device_id_type=MESH)))
         return made
 
@@ -315,19 +308,22 @@
             def _():
                 copy.start()
 
-    def finish_recv(made, recv):
-        for at, (ds, dg) in enumerate(steps[:len(made)]):
-            back = made[at ^ 1 if at < 4 else 11 - at][2]
-
+    def take(tiles, sem):
+        block = blanks.at[pl.ds(0, tiles)]
+        pltpu.make_async_copy(block, block, sem).wait()
+
+    def finish_recv(recv, slab_tiles, grp_tiles):
+        for at, (ds, dg) in enumerate(steps[:4]):
             @pl.when(inside(ds, dg))
             def _():
-                back.wait_recv()
-
-    def finish_send(made):
-        for ds, dg, copy in made:
+                if (slab_tiles if ds else grp_tiles):
+                    take(slab_tiles if ds else grp_tiles, recv.at[at])
+
+    def finish_send(slab_tiles, grp_tiles, corner_tiles):
+        for at, (ds, dg) in enumerate(steps):
             @pl.when(inside(ds, dg))
             def _():
-                copy.wait_send()
+                take(corner_tiles if ds and dg else slab_tiles if ds else grp_tiles, sends.at[at])
 
     def blank(dst_a, land):
         zero_a = jnp.zeros((dst_a.shape[0], HALO) + dst_a.shape[2:], jnp.float32)
@@ -393,12 +389,14 @@
         pack(s1, 6, i, e1a[6, HALO + 2 * i], e1a[6, HALO + 2 * i + 1])
         return 0
 
-    for at in range(4, 7):
-        fetched[at].wait()
+    take(9 * X, isem.at[4])
     lax.fori_loop(0, X // 2, own, 0)
     blank(e1a, h1)
     blank(e2a, h2)
     blank(rqa, h3)
+    for ch in range(6):
+        for x in (HALO - REACH, HALO + X + REACH - 1):
+            rqb[ch, x] = jnp.zeros((8, 128), jnp.float32)
 
     zrows = Z // ns
 
@@ -411,7 +409,7 @@
         for m in reversed(range(1, ns)):
             to = mirrored(si, m, ns)
             pltpu.make_async_remote_copy(
-                src_ref=source.at[to], dst_ref=target.at[si], send_sem=tsend.at[at], recv_sem=trecv.at[at],
+                src_ref=source.at[to], dst_ref=target.at[si], send_sem=tsend.at[0 if at < 6 else 1], recv_sem=trecv.at[at],
                 device_id=(to, gi), device_id_type=MESH).start()
 
     def landed(target, sem):
@@ -468,7 +466,7 @@
             side, end = (0 if dg < 0 else 1), (0 if ds < 0 else 1)
             made.append((ds, dg, pltpu.make_async_remote_copy(
                 src_ref=ftake.at[side, end], dst_ref=fland.at[side, 1 - end],
-                send_sem=sendf.at[at], recv_sem=recvf.at[3 - at],
+                send_sem=sends.at[4 + at], recv_sem=recvf.at[3 - at],
                 device_id=(si + ds, gi + dg), device_id_type=MESH)))
         return made
 
@@ -492,7 +490,7 @@
             pair = HALO // 2 + X // 2 if ds < 0 else HALO // 2 - 1
             made.append((ds, dg, pltpu.make_async_remote_copy(
                 src_ref=k3.at[side, end], dst_ref=h3.at[side, :, pl.ds(pair, 1)],
-                send_sem=sendk.at[at], recv_sem=recvk.at[3 - at],
+                send_sem=sends.at[4 + at], recv_sem=recvk.at[3 - at],
                 device_id=(si + ds, gi + dg), device_id_type=MESH)))
         return made
 
@@ -502,7 +500,7 @@
             side, end = (0 if dg < 0 else 1), (0 if ds < 0 else 1)
             made.append((ds, dg, pltpu.make_async_remote_copy(
                 src_ref=ctake.at[side, end], dst_ref=cland.at[side, 1 - end],
-                send_sem=csend.at[at], recv_sem=crecv.at[3 - at],
+                send_sem=sends.at[4 + at], recv_sem=crecv.at[3 - at],
                 device_id=(si + ds, gi + dg), device_id_type=MESH)))
         return made
 
@@ -551,15 +549,15 @@
                         h1[side, right[1], pair] = pltpu.roll(tile, 5 if side else 1, 0)
 
     corners = corner_copies()
-    zeroth = copies(e1a, e1a, s1, h1, send0, recv0, 6, 7, 4, REACH - 1)
-    first = copies(e1a, e1a, s1, h1, send1, recv1, 0, 3, 4, REACH - 1)
-    rest = copies(e1a, e1a, s1, h1, send4, recv4, 3, 6, 4, REACH - 1, None, ends)
-    late = (copies(e1a, e1a, s1, h1, sendu, recvu, 0, 3, 2, 1, REACH),
-            copies(e1a, e1a, s1, h1, sendw, recvw, 6, 7, 2, 1, REACH))
-    second = copies(e2a, e2a, s2, h2, send2, recv2, 0, 3, 4, REACH - 1)
+    zeroth = copies(e1a, e1a, s1, h1, recv0, 6, 7, 4, REACH - 1)
+    first = copies(e1a, e1a, s1, h1, recv1, 0, 3, 4, REACH - 1)
+    rest = copies(e1a, e1a, s1, h1, recv1, 3, 6, 4, REACH - 1, None, ends)
+    late = (copies(e1a, e1a, s1, h1, recv2, 0, 3, 2, 1, REACH),
+            copies(e1a, e1a, s1, h1, recv2, 6, 7, 2, 1, REACH))
+    second = copies(e2a, e2a, s2, h2, recv2, 0, 3, 4, REACH - 1)
     tips = tip_copies()
-    third = copies(rqa, rqa, s3, h3, send3, recv3, 0, 3, 4, 1, REACH)
-    outer = copies(rqa, rqa, s3, h3, sendq, recvq, 3, 6, 2, REACH - 1, REACH)
+    third = copies(rqa, rqa, s3, h3, recv3, 0, 3, 4, 1, REACH)
+    outer = copies(rqa, rqa, s3, h3, recv3, 3, 6, 2, REACH - 1, REACH)
     wedges = wedge_copies()
     meet(barrier, 1)
     begin(zeroth)
@@ -573,7 +571,7 @@
     for at in range(len(rounds) - 2):
         meet(known.at[at], rounds[at])
         greet(known.at[at + 1], rounds[at + 1])
-    finish_recv(zeroth, recv0)
+    finish_recv(recv0, REACH - 1, X // 2)
     corner_unpack(corners)
     meet(known.at[len(rounds) - 2], rounds[-2])
     greet(known.at[len(rounds) - 1], rounds[-1])
@@ -639,11 +637,10 @@
 
     edge_link(HALO - 2)
     over_rows(HALO - 1, HALO + X + 1, WIDE_K, all_coefficients)
-    finish_recv(first, recv1)
-    finish_recv(rest, recv4)
+    finish_recv(recv1, 6 * (REACH - 1), 3 * X)
     lax.fori_loop(0, (X + 2 * HALO) // 2, open1, 0)
 
-    def operate(x, va, vb, base, both=True):
+    def operate(x, va, vb, base, chosen=slice(0, 2)):
         result = []
         coef = [[kc[j, x] for j in range(5)] + [kc[0, x - 1]] for kc in (kca, kcb)]
         for c in range(3):
@@ -652,7 +649,7 @@
             la, lb = down_y(a, b)
             pair = []
             halves = ((a, va, ua, la, coef[0], dga), (b, vb, ub, lb, coef[1], dgb))
-            for v, ref, u, l, k, dg in halves if both else halves[:1]:
+            for v, ref, u, l, k, dg in halves[chosen]:
                 parts = (
                     k[0] * ref[base + c, x + 1] + k[5] * ref[base + c, x - 1],
                     k[1] * u + k[2] * l,
@@ -663,18 +660,17 @@
             result.append(pair)
         return result
 
-    def solve(step, va, vb, rhs_of, reach, ship_halo=None):
-        def residual(rows_here, _):
-            for x in rows_here:
-                image = operate(x, va, vb, 0)
-                for c in range(3):
-                    ra, rb = rhs_of(c, x)
-                    rqa[c, x] = ra - image[c][0]
-                    rqb[c, x] = rb - image[c][1]
-            return 0
-
-        over_rows(HALO - reach, HALO + X + reach, WIDE_R, residual)
-
+    only_a, only_b = slice(0, 1), slice(1, 2)
+
+    def residual(rows_here, _):
+        for x in rows_here:
+            image = operate(x, e1a, e1b, 0)
+            for c in range(3):
+                rqa[c, x] = e1a[3 + c, x] - image[c][0]
+                rqb[c, x] = e1b[3 + c, x] - image[c][1]
+        return 0
+
+    def solve(step, ship_halo=None):
         def put(x, image):
             for c in range(3):
                 rqa[3 + c, x] = image[c][0]
@@ -703,9 +699,11 @@
         def centred(rows_here, sums):
             ww, wr, mix, wt = sums
             for x in rows_here:
-                image = operate(x, rqa, rqb, 3, False)
+                image = operate(x, rqa, rqb, 3, only_a)
                 for c in range(3):
                     r, q, s = rqa[c, x], rqa[3 + c, x], image[c][0]
+                    if step == 0:
+                        sa[c, x] = s
                     w, t = q - mu * r, s - mu * q
                     ww, wr, mix, wt = ww + w * w, wr + w * r, mix + (r * t + w * q), wt + w * t
             return ww, wr, mix, wt
@@ -722,7 +720,7 @@
             meet(known.at[len(rounds) - 1], rounds[-1])
         for other in others:
             pltpu.make_async_remote_copy(
-                src_ref=gath.at[step, me], dst_ref=gath.at[step, me], send_sem=asend.at[step], recv_sem=arecv.at[step],
+                src_ref=gath.at[step, me], dst_ref=gath.at[step, me], send_sem=asend, recv_sem=arecv.at[step],
                 device_id=other, device_id_type=MESH).start()
 
     def collect(step):
@@ -743,9 +741,9 @@
         beta = after / (curved - ratio * after / alpha)
         return jnp.broadcast_to(alpha + beta * (1.0 + ratio), (8, 128)), jnp.broadcast_to(-beta * alpha, (8, 128))
 
-    def drain(step):
-        block = gath.at[step, pl.ds(0, count - 1)]
-        pltpu.make_async_copy(block, block, asend.at[step]).wait()
+    def drain():
+        block = gath.at[:, pl.ds(0, count - 1)]
+        pltpu.make_async_copy(block, block, asend).wait()
 
     def joined(c, x, near, far):
         r, q = rqa[c, x], rqa[3 + c, x]
@@ -775,12 +773,11 @@
 
     outer_residual(HALO - 2)
     outer_residual(HALO + X + 1)
-    solve(0, e1a, e1b, lambda c, x: (e1a[3 + c, x], e1b[3 + c, x]), 1, ship_halo)
+    over_rows(HALO - 1, HALO + X + 1, WIDE_R, residual)
+    solve(0, ship_halo)
     spread_out(outb.at[3], inb.at[3], 3)
-    finish_recv(second, recv2)
+    finish_recv(recv2, 3 * (REACH - 1) + 4, 3 * X // 2)
     tip_unpack(tips)
-    for made, recv in zip(late, (recvu, recvw)):
-        finish_recv(made, recv)
     edge_link(HALO - REACH)
     coefficients(HALO - 2)
     coefficients(HALO + X + 1)
@@ -791,7 +788,7 @@
         return 0
 
     lax.fori_loop(0, (X + 2 * HALO) // 2, open2, 0)
-    finish_recv(third, recv3)
+    finish_recv(recv3, 3 + 3 * (REACH - 1), 3 * X // 2)
     for at, (ds, dg) in enumerate(steps[4:]):
         back = wedges[3 - at][2]
 
@@ -814,33 +811,36 @@
                     split(c, 2 * pair + o, tile, 1, 6, 2)
                 else:
                     split(c, 2 * pair + o, tile, 0, 5, 3)
-    finish_recv(outer, recvq)
+    finish_send(13 * (REACH - 1) + 7, 13 * X // 2, 6)
+    for x in range(HALO - 1, HALO + X + 1):
+        image = operate(x, rqa, rqb, 3, only_b)
+        for c in range(3):
+            sb[c, x] = image[c][0]
+            e2a[c, x] = MASS_TERM * e1a[c, x] + e2a[c, x] - e1a[3 + c, x] + rqa[c, x]
+            e2b[c, x] = MASS_TERM * e1b[c, x] + e2b[c, x] - e1b[3 + c, x] + rqb[c, x]
+    for x in (HALO - 2, HALO + X + 1):
+        image = operate(x, e1a, e1b, 0, only_a)
+        for c in range(3):
+            e2a[c, x] = MASS_TERM * e1a[c, x] + e2a[c, x] - image[c][0]
+    for x in (HALO - 2, HALO - 1, HALO + X, HALO + X + 1):
+        image = operate(x, rqa, rqb, 3, only_a)
+        for c in range(3):
+            sa[c, x] = image[c][0]
     c0, c1 = collect(0)
 
-    def step1(x, both=True):
+    def step1(x, base, rq, g, s, u1, comps):
         for c in range(3):
-            u1a[c, x] = e1a[c, x] + (c0 * rqa[c, x] + c1 * rqa[3 + c, x])
-            u1b[c, x] = e1b[c, x] + (c0 * rqb[c, x] + c1 * rqb[3 + c, x]) if both else jnp.zeros((8, 128), jnp.float32)
-
-    for x in range(HALO - REACH + 1, HALO + X + REACH - 1):
-        step1(x)
-    step1(HALO - REACH, False)
-    step1(HALO + X + REACH - 1, False)
-    finish_send(zeroth)
-    finish_send(corners)
-    finish_send(rest)
-    finish_send(first)
-    finish_send(second)
-    finish_send(tips)
-    for made in late:
-        finish_send(made)
-    finish_send(third)
-    finish_send(outer)
-    finish_send(wedges)
-
-    def rhs2(c, x):
-        return (MASS_TERM * (2.0 * u1a[c, x] - e1a[c, x]) + e2a[c, x],
-                MASS_TERM * (2.0 * u1b[c, x] - e1b[c, x]) + e2b[c, x])
+            r, q = rq[c, x], rq[3 + c, x]
+            grown = c0 * r + c1 * q
+            if c in comps:
+                u1[c, x] = base[c, x] + grown
+            rq[c, x] = g[c, x] + (2.0 * MASS_TERM) * grown - (c0 * q + c1 * s[c, x])
+
+    for x in range(HALO - 2, HALO + X + 2):
+        own_row = HALO <= x < HALO + X
+        step1(x, e1a, rqa, e2a, sa, u1a, (0, 1, 2) if own_row else ())
+        if HALO - 1 <= x <= HALO + X:
+            step1(x, e1b, rqb, e2b, sb, u1b, (1,) if own_row else ())
 
     def early(at, ref, ch):
         for x in range(X):
@@ -849,8 +849,8 @@
         spread_out(outb.at[at], inb.at[at], at)
         inb[at, si] = outb[at, si]
 
+    solve(1)
     early(2, u1a, 2)
-    solve(1, u1a, u1b, rhs2, 2)
     early(4, rqa, 2)
     early(5, rqa, 5)
     c0, c1 = collect(1)
@@ -890,7 +890,7 @@
             before = pltpu.roll(joint(outb, j - 1, zrows - 8, zrows), 5, 0) if j else zero
             after = pltpu.roll(joint(outb, j + 1, 0, 8), 5, 0) if j + 1 < ns else zero
             outx[j] = jnp.where(sub == 4, before, jnp.where(sub == 5, after, tile))
-        spread_out(outx, inx, 6)
+        spread_out(outx.at[:, pl.ds(0, 6)], inx.at[:, pl.ds(0, 6)], 6)
         inx[si] = outx[si]
 
     finish(0)
@@ -936,7 +936,7 @@
     wide = lax.broadcasted_iota(jnp.int32, (zrows, 128), 1)
     encode(3, [scale[y] * (jnp.where(wide < 127, up_z(field[y]), 0.0) - jnp.where(wide > 0, down_z(field[y]), 0.0))
                for y in range(Y)])
-    landed(inx, trecv.at[6])
+    landed(inx.at[:, pl.ds(0, 6)], trecv.at[6])
     edges = regroup([inx[j] for j in range(ns)])
     stress = []
     for y in range(Y):
@@ -955,11 +955,10 @@
         outside.append(jnp.concatenate([jnp.where(upper, quarter[q], pltpu.roll(quarter[q + 1], 4, 0)) for q in (0, 2)], axis=0))
     field = [outside[0]] + field + [outside[1]]
     encode(4, [scale[y] * (field[y + 2] - field[y]) for y in range(Y)])
-    drain(0)
-    drain(1)
-    for at in range(6):
-        landed(inb.at[at], tsend.at[at])
-    landed(inx, tsend.at[6])
+    drain()
+    block = inb.at[:, pl.ds(0, ns - 1)]
+    pltpu.make_async_copy(block, block, tsend.at[0]).wait()
+    landed(inx.at[:, pl.ds(0, 6)], tsend.at[1])
 
 
 def store(disp_in, coef_in, disp_out, coef_out, sems):
@@ -1004,16 +1003,15 @@
         scratch_shapes=[
             vm(*u_now.shape), vm(*u_now.shape), vm(*u_now.shape), vm(*stiffness.shape),
             pltpu.VMEM(broken.shape, broken.dtype), pltpu.VMEM(flags.shape, flags.dtype),
-            vm(*ez.shape), pltpu.VMEM(gt.shape, gt.dtype), pltpu.SemaphoreType.DMA((8,)),
+            vm(*ez.shape), pltpu.VMEM(gt.shape, gt.dtype), pltpu.SemaphoreType.DMA((6,)),
             ext(7), ext(7), stage(7), land(7),
             ext(3), ext(3), stage(3), land(3),
             ext(6), ext(6), stage(3), land(3), vm(2, 2, 3, 1, Y, Z), vm(2, 3, 2, Y, Z),
-            ext(3), ext(3), vm(Y, zrows, X * ns), ext(3), ext(3), ext(5), ext(5),
-            pltpu.SemaphoreType.REGULAR((4,)), vm(2, ns * ng, 1, 128), vm(7, Y * X, Z), vm(6, ns, zrows, 128), vm(6, ns, zrows, 128), vm(ns, 8, 128), vm(ns, 8, 128), vm(6, Y * zrows, X * ns),
-            vm(2, 2, 2, Y, Z), vm(2, 2, 2, Y, Z), dma((4,)), dma((4,)), dma((4,)), dma((4,)),
-            dma((4,)), dma((4,)), dma((4,)), dma((4,)), dma((4,)), dma((4,)), dma((4,)), dma((4,)), dma((2,)), dma((2,)), dma((4,)), dma((4,)),
-            dma((2,)), dma((2,)), dma((2,)), dma((2,)), vm(2, 2, Y, Z), vm(2, 2, Y, Z), dma((4,)), dma((4,)),
-            dma((2,)), dma((2,)), dma((7,)), dma((7,)),
+            ext(3), ext(3), ext(3), ext(3), vm(Y, zrows, X * ns), ext(3), ext(3), ext(5), ext(5),
+            pltpu.SemaphoreType.REGULAR((3,)), vm(2, ns * ng, 1, 128), vm(7, Y * X, Z), vm(6, ns, zrows, 128), vm(6, ns, zrows, 128), vm(ns, 8, 128), vm(ns, 8, 128), vm(6, Y * zrows, X * ns),
+            vm(max(9 * X, 13 * X // 2), Y, Z), dma((8,)), vm(2, 2, 2, Y, Z), vm(2, 2, 2, Y, Z), dma((4,)),
+            dma((4,)), dma((4,)), dma((4,)), dma((4,)), dma((4,)), vm(2, 2, Y, Z), vm(2, 2, Y, Z), dma((4,)),
+            dma, dma((2,)), dma((2,)), dma((7,)),
         ],
         compiler_params=pltpu.CompilerParams(collective_id=0, has_side_effects=True, vmem_limit_bytes=24 << 20),
     )(*operands)

time: 31.2 us -> 30.5 us (0.978)
  Pallas kernels: 30.4 us -> 29.7 us
    pallas_call x1, Pallas kernels: 29.6 us -> 28.9 us  [fused(): pl.pallas_call(lambda *refs: kernel(ns, ng, *refs), name='lattice', out_s...]
where the time goes in v9:
time: 30.5 us; the launch traced here: 30.3 us
  Pallas kernels  29.7 us (97%)
  between operations  0.64 us (2%)
    pallas_call x1, Pallas kernels, fused(): pl.pallas_call(lambda *refs: kernel(ns, ng, *refs), name='lattice', out_s...  28.9 us
    pallas_call x1, Pallas kernels, fused(): pl.pallas_call(store, name='store', out_shape=tuple((jax.ShapeDtypeStruct...  0.83 us

profile of v9, /device:TPU:0, one launch (start us, length us, event | category | flops | bytes accessed | tf_op | source)
XLA Modules:
  0.0 30.3 jit_solution(9757469485139765039)
XLA Ops:
  0.6 28.9 %lattice.1 = (f32[3,16,8,128]{3,2,1,0:T(8,128)S(1)}, f32[6,128,128]{2,1,0:T(8,128)S(1)}) custom-call(f32[3,16,8,128]{3,2,1,0:T(8,128)} %refs_0_.1, f32[3,16,8,128]{3,2,1,0:T(8,128)} %refs_1_.1, f32[3,16,8,128]{3,2,1,0:T(8,128)} %refs_2_.1, f32[16,8,128]{2,1,0:T(8,128)} %refs_3_.1, s32[4,2,32]{2,1,0:T(2,128)} %refs_4_.1, s32[4,2,32]{2,1,0:T(2,128)} %refs_5_.1, ...), custom_call_target="tpu_custom_call" | custom-call | tf_op jit(solution)/shard_map/lattice/pallas_call | solution.py:997
  29.5 0.8 %store.1 = (f32[3,16,8,128]{3,2,1,0:T(8,128)}, f32[6,128,128]{2,1,0:T(8,128)}) custom-call(f32[3,16,8,128]{3,2,1,0:T(8,128)S(1)} %get-tuple-element.6.disp_in, f32[6,128,128]{2,1,0:T(8,128)S(1)} %get-tuple-element.7.coef_in), custom_call_target="tpu_custom_call" | custom-call | tf_op jit(solution)/shard_map/store/pallas_call | solution.py:1018

commit v10 on v9

--- a/solution.py
+++ b/solution.py
@@ -406,8 +406,8 @@
             out[j] = turned[j * zrows:(j + 1) * zrows]
 
     def spread_out(source, target, at):
-        for m in reversed(range(1, ns)):
-            to = mirrored(si, m, ns)
+        for m in range(1, ns):
+            to = lax.rem(si + m, ns)
             pltpu.make_async_remote_copy(
                 src_ref=source.at[to], dst_ref=target.at[si], send_sem=tsend.at[0 if at < 6 else 1], recv_sem=trecv.at[at],
                 device_id=(to, gi), device_id_type=MESH).start()
@@ -775,7 +775,6 @@
     outer_residual(HALO + X + 1)
     over_rows(HALO - 1, HALO + X + 1, WIDE_R, residual)
     solve(0, ship_halo)
-    spread_out(outb.at[3], inb.at[3], 3)
     finish_recv(recv2, 3 * (REACH - 1) + 4, 3 * X // 2)
     tip_unpack(tips)
     edge_link(HALO - REACH)
@@ -812,6 +811,7 @@
                 else:
                     split(c, 2 * pair + o, tile, 0, 5, 3)
     finish_send(13 * (REACH - 1) + 7, 13 * X // 2, 6)
+    spread_out(outb.at[3], inb.at[3], 3)
     for x in range(HALO - 1, HALO + X + 1):
         image = operate(x, rqa, rqb, 3, only_b)
         for c in range(3):

time: 30.5 us -> 30.1 us (0.987)
  Pallas kernels: 29.7 us -> 29.2 us
    pallas_call x1, Pallas kernels: 28.9 us -> 28.4 us  [fused(): pl.pallas_call(lambda *refs: kernel(ns, ng, *refs), name='lattice', out_s...]
where the time goes in v10:
time: 30.1 us; the launch traced here: 29.9 us
  Pallas kernels  29.2 us (97%)
  between operations  0.64 us (2%)
    pallas_call x1, Pallas kernels, fused(): pl.pallas_call(lambda *refs: kernel(ns, ng, *refs), name='lattice', out_s...  28.4 us
    pallas_call x1, Pallas kernels, fused(): pl.pallas_call(store, name='store', out_shape=tuple((jax.ShapeDtypeStruct...  0.83 us

profile of v10, /device:TPU:0, one launch (start us, length us, event | category | flops | bytes accessed | tf_op | source)
XLA Modules:
  0.0 29.9 jit_solution(10476482474685396641)
XLA Ops:
  0.6 28.4 %lattice.1 = (f32[3,16,8,128]{3,2,1,0:T(8,128)S(1)}, f32[6,128,128]{2,1,0:T(8,128)S(1)}) custom-call(f32[3,16,8,128]{3,2,1,0:T(8,128)} %refs_0_.1, f32[3,16,8,128]{3,2,1,0:T(8,128)} %refs_1_.1, f32[3,16,8,128]{3,2,1,0:T(8,128)} %refs_2_.1, f32[16,8,128]{2,1,0:T(8,128)} %refs_3_.1, s32[4,2,32]{2,1,0:T(2,128)} %refs_4_.1, s32[4,2,32]{2,1,0:T(2,128)} %refs_5_.1, ...), custom_call_target="tpu_custom_call" | custom-call | tf_op jit(solution)/shard_map/lattice/pallas_call | solution.py:997
  29.0 0.8 %store.1 = (f32[3,16,8,128]{3,2,1,0:T(8,128)}, f32[6,128,128]{2,1,0:T(8,128)}) custom-call(f32[3,16,8,128]{3,2,1,0:T(8,128)S(1)} %get-tuple-element.6.disp_in, f32[6,128,128]{2,1,0:T(8,128)S(1)} %get-tuple-element.7.coef_in), custom_call_target="tpu_custom_call" | custom-call | tf_op jit(solution)/shard_map/store/pallas_call | solution.py:1018

commit v11 on v10

--- a/solution.py
+++ b/solution.py
@@ -767,9 +767,9 @@
                 even, odd = [joined(c, x + o, 2, 6) if o == end else joined(c, x + o, 3, 5) for o in range(2)]
                 k3[0, end, c, 0] = jnp.where(upper, even, pltpu.roll(odd, 4, 0))
                 k3[1, end, c, 0] = jnp.where(upper, pltpu.roll(even, 4, 0), odd)
-        begin(third)
         begin(wedges)
         begin(outer)
+        begin(third)
 
     outer_residual(HALO - 2)
     outer_residual(HALO + X + 1)

time: 30.1 us -> 29.8 us (0.990)
  no operation moved by 1% of the time
where the time goes in v11:
time: 29.8 us; the launch traced here: 29.6 us
  Pallas kernels  29 us (97%)
  between operations  0.64 us (2%)
    pallas_call x1, Pallas kernels, fused(): pl.pallas_call(lambda *refs: kernel(ns, ng, *refs), name='lattice', out_s...  28.2 us
    pallas_call x1, Pallas kernels, fused(): pl.pallas_call(store, name='store', out_shape=tuple((jax.ShapeDtypeStruct...  0.83 us

profile of v11, /device:TPU:0, one launch (start us, length us, event | category | flops | bytes accessed | tf_op | source)
XLA Modules:
  0.0 29.6 jit_solution(14593504750255259198)
XLA Ops:
  0.6 28.2 %lattice.1 = (f32[3,16,8,128]{3,2,1,0:T(8,128)S(1)}, f32[6,128,128]{2,1,0:T(8,128)S(1)}) custom-call(f32[3,16,8,128]{3,2,1,0:T(8,128)} %refs_0_.1, f32[3,16,8,128]{3,2,1,0:T(8,128)} %refs_1_.1, f32[3,16,8,128]{3,2,1,0:T(8,128)} %refs_2_.1, f32[16,8,128]{2,1,0:T(8,128)} %refs_3_.1, s32[4,2,32]{2,1,0:T(2,128)} %refs_4_.1, s32[4,2,32]{2,1,0:T(2,128)} %refs_5_.1, ...), custom_call_target="tpu_custom_call" | custom-call | tf_op jit(solution)/shard_map/lattice/pallas_call | solution.py:997
  28.8 0.8 %store.1 = (f32[3,16,8,128]{3,2,1,0:T(8,128)}, f32[6,128,128]{2,1,0:T(8,128)}) custom-call(f32[3,16,8,128]{3,2,1,0:T(8,128)S(1)} %get-tuple-element.6.disp_in, f32[6,128,128]{2,1,0:T(8,128)S(1)} %get-tuple-element.7.coef_in), custom_call_target="tpu_custom_call" | custom-call | tf_op jit(solution)/shard_map/store/pallas_call | solution.py:1018

commit v12 on v11

--- a/solution.py
+++ b/solution.py
@@ -391,13 +391,6 @@
 
     take(9 * X, isem.at[4])
     lax.fori_loop(0, X // 2, own, 0)
-    blank(e1a, h1)
-    blank(e2a, h2)
-    blank(rqa, h3)
-    for ch in range(6):
-        for x in (HALO - REACH, HALO + X + REACH - 1):
-            rqb[ch, x] = jnp.zeros((8, 128), jnp.float32)
-
     zrows = Z // ns
 
     def turn_out(value, out):
@@ -566,6 +559,13 @@
     inner_ends()
     begin(rest)
     greet(known.at[0], rounds[0])
+    blank(e1a, h1)
+    blank(e2a, h2)
+    blank(rqa, h3)
+    for ch in range(6):
+        for x in (HALO - REACH, HALO + X + REACH - 1):
+            rqb[ch, x] = jnp.zeros((8, 128), jnp.float32)
+
     turn_out(rows[3], outb.at[3])
     inb[3, si] = outb[3, si]
     for at in range(len(rounds) - 2):

time: 29.8 us -> 29.8 us (level)
  no operation moved by 1% of the time
where the time goes in v12:
time: 29.8 us; the launch traced here: 29.7 us
  Pallas kernels  29 us (97%)
  between operations  0.64 us (2%)
    pallas_call x1, Pallas kernels, fused(): pl.pallas_call(lambda *refs: kernel(ns, ng, *refs), name='lattice', out_s...  28.2 us
    pallas_call x1, Pallas kernels, fused(): pl.pallas_call(store, name='store', out_shape=tuple((jax.ShapeDtypeStruct...  0.83 us

profile of v12, /device:TPU:0, one launch (start us, length us, event | category | flops | bytes accessed | tf_op | source)
XLA Modules:
  0.0 29.7 jit_solution(5499538023074107191)
XLA Ops:
  0.6 28.2 %lattice.1 = (f32[3,16,8,128]{3,2,1,0:T(8,128)S(1)}, f32[6,128,128]{2,1,0:T(8,128)S(1)}) custom-call(f32[3,16,8,128]{3,2,1,0:T(8,128)} %refs_0_.1, f32[3,16,8,128]{3,2,1,0:T(8,128)} %refs_1_.1, f32[3,16,8,128]{3,2,1,0:T(8,128)} %refs_2_.1, f32[16,8,128]{2,1,0:T(8,128)} %refs_3_.1, s32[4,2,32]{2,1,0:T(2,128)} %refs_4_.1, s32[4,2,32]{2,1,0:T(2,128)} %refs_5_.1, ...), custom_call_target="tpu_custom_call" | custom-call | tf_op jit(solution)/shard_map/lattice/pallas_call | solution.py:997
  28.8 0.8 %store.1 = (f32[3,16,8,128]{3,2,1,0:T(8,128)}, f32[6,128,128]{2,1,0:T(8,128)}) custom-call(f32[3,16,8,128]{3,2,1,0:T(8,128)S(1)} %get-tuple-element.6.disp_in, f32[6,128,128]{2,1,0:T(8,128)S(1)} %get-tuple-element.7.coef_in), custom_call_target="tpu_custom_call" | custom-call | tf_op jit(solution)/shard_map/store/pallas_call | solution.py:1018
